TPU v7x, 512 devices: a whole 4x4x16 slice. The times are simulated.
512 devices in a mesh: shot: 8 (over x, core), chan: 64 (over y, z).
Axes of the slice: x: 4, y: 4, z: 16, core: 2. Of those that a mesh axis runs over, the one named last changes fastest.
Arguments:
- traces: float32 [32, 1024, 4096], P('shot', 'chan'), may hold values from -6 to 6
- shifts: int32 [32, 1024], P('shot', 'chan'), may hold values from 0 to 1023
- aperture_lo: int32 [1024], P('chan'), may hold values from 0 to 15
- aperture_hi: int32 [1024], P('chan'), may hold values from 17 to 32
- dip_band: int32 [1024], P('chan'), may hold values from 64 to 512
Outputs:
- filtered: float32 [32, 1024, 4096], P(None, ('chan', 'shot'))
All inputs are finite; a program needn't handle non-finite values.
Results may differ from a plain program's by a relative error of at most 0.0003.
Values sent between devices are 32-bit elements; how exact they have to be, the bound alone decides.
No kernel may reach another device: no remote copies, remote signals or barrier semaphores. Data moves between devices by JAX's collectives and lax.ppermute only.
A program may use at most 64 MiB of HBM per device.

v0:
```python
import functools

import jax
import jax.numpy as jnp
import numpy as np
from jax import lax
from jax.experimental import pallas as pl
from jax.experimental.pallas import tpu as pltpu
from jax.sharding import PartitionSpec as P

LANES = 128
HALF = 5
HALO = 2 * HALF
HIGHEST = lax.Precision.HIGHEST


def whole(space=pltpu.VMEM):
    return pl.BlockSpec(memory_space=space)


def align_kernel(dims, shifts_ref, traces_ref, down_ref, up_ref, held, sems):
    shots, chans, rows = dims
    tiles = chans * rows
    for shot in range(shots):
        pltpu.make_async_copy(
            traces_ref.at[pl.ds(shot * tiles, tiles)], held.at[pl.ds(shot * tiles, tiles)], sems.at[shot]
        ).start()
    held[pl.ds(shots * tiles, held.shape[0] - shots * tiles), :] = jnp.zeros(
        (held.shape[0] - shots * tiles, LANES), jnp.float32
    )
    lane = lax.broadcasted_iota(jnp.int32, (rows, LANES), 1)
    sample = lax.broadcasted_iota(jnp.int32, (rows, LANES), 0) * LANES + lane
    for shot in range(shots):
        pltpu.make_async_copy(
            traces_ref.at[pl.ds(shot * tiles, tiles)], held.at[pl.ds(shot * tiles, tiles)], sems.at[shot]
        ).wait()
    for shot in range(shots):
        for chan in range(chans):
            shift = shifts_ref[shot, chan]
            whole_rows, part = shift // LANES, shift % LANES
            base = shot * tiles + (chan // 8) * (rows * 8) + chan % 8
            first = held[pl.ds(base + whole_rows * 8, rows, stride=8), :]
            second = held[pl.ds(base + whole_rows * 8 + 8, rows, stride=8), :]
            mixed = jnp.where(lane >= part, first, second)
            moved = pltpu.roll(mixed, (LANES - part) % LANES, 1)
            moved = jnp.where(sample < rows * LANES - shift, moved, 0.0)
            if chan < HALO:
                down_ref[shot, chan] = moved
            if chan >= chans - HALO:
                up_ref[shot, chan - (chans - HALO)] = moved


def align(traces, shifts):
    shots, chans, length = traces.shape
    rows = length // LANES
    flat = traces.reshape(shots, chans // 8, 8, rows, LANES).transpose(0, 1, 3, 2, 4).reshape(-1, LANES)
    edge = jax.ShapeDtypeStruct((shots, HALO, rows, LANES), jnp.float32)
    pad = 8 * 9
    return pl.pallas_call(
        functools.partial(align_kernel, (shots, chans, rows)),
        out_shape=(edge, edge),
        in_specs=[whole(pltpu.SMEM), whole(pl.ANY)],
        out_specs=(whole(), whole()),
        scratch_shapes=[
            pltpu.VMEM((shots * chans * rows + pad, LANES), jnp.float32),
            pltpu.SemaphoreType.DMA((shots,)),
        ],
        name="align",
    )(shifts, flat)


def order(a, b):
    return jnp.minimum(a, b), jnp.maximum(a, b)


def medians(values, count):
    total = len(values)
    pairs = {}
    blocks = {}

    def pair(start):
        if start not in pairs:
            pairs[start] = order(values[start], values[start + 1])
        return pairs[start]

    def block(start):
        if start not in blocks:
            (a, b), (c, d) = pair(start), pair(start + 2)
            low, m = order(a, c)
            n, high = order(b, d)
            m, n = order(m, n)
            blocks[start] = (low, m, n, high)
        return blocks[start]

    result = []
    for group in range(-1, (count + 3) // 4):
        wanted = [w for w in range(4 * group + 1, 4 * group + 5) if 0 <= w < count]
        if not wanted:
            continue
        a1, a2, a3, a4 = block(4 * group + 4)
        b1, b2, b3, b4 = block(4 * group + 8)
        t, u = jnp.maximum(a1, b1), jnp.minimum(a3, b3)
        c4 = jnp.maximum(a3, b3)
        c2, c3 = order(t, u)
        d1 = jnp.minimum(a2, b2)
        t, u = jnp.maximum(a2, b2), jnp.minimum(a4, b4)
        d2, d3 = order(t, u)
        m3, (m4, m5), m6 = jnp.maximum(d1, c2), order(d2, c3), jnp.minimum(d3, c4)
        for half, extra in ((0, 4 * group + 2), (1, 4 * group + 12)):
            mine = [w for w in wanted if (w - 4 * group - 1) // 2 == half]
            if not mine:
                continue
            p, q = pair(extra)
            s5 = jnp.minimum(m5, jnp.minimum(jnp.maximum(m4, p), jnp.maximum(m3, q)))
            s6 = jnp.minimum(m6, jnp.minimum(jnp.maximum(m5, p), jnp.maximum(m4, q)))
            for w in mine:
                lone = extra - 1 if (w - 4 * group - 1) == 0 else extra + 2 if (w - 4 * group - 1) == 3 else (
                    4 * group + 12 if half == 0 else 4 * group + 3
                )
                assert w <= lone <= w + 10 and lone < total
                result.append(jnp.maximum(s5, jnp.minimum(s6, values[lone])))
    assert len(result) == count
    return result


def clean_kernel(dims, shifts_ref, low_ref, high_ref, left_ref, down_ref, up_ref, right_ref, out_ref, held):
    shots, chans, rows = dims
    first_shot = lax.axis_index("shot") * shots
    lead = 8
    for chan in range(chans):
        held[chan, pl.ds(0, lead), :] = jnp.zeros((lead, LANES), jnp.float32)
    lane = lax.broadcasted_iota(jnp.int32, (rows, LANES), 1)

    def one_shot(shot, carry):
        def one_part(part, inner):
            place = pl.ds(pl.multiple_of(part * 8, 8), 8)
            values = [left_ref[shot, i, place, :] for i in range(HALO)]
            values += [down_ref[shot, i, place, :] for i in range(HALO)]
            values += [up_ref[shot, i, place, :] for i in range(2 * HALO - chans, HALO)]
            values += [right_ref[shot, i, place, :] for i in range(HALO)]
            once = medians(values, chans + HALO)
            once = [values[HALF + i] - once[i] for i in range(chans + HALO)]
            twice = medians(once, chans)
            stored = pl.ds(pl.multiple_of(lead + part * 8, 8), 8)
            for i in range(chans):
                held[i, stored, :] = once[HALF + i] - twice[i]
            return inner

        lax.fori_loop(0, rows // 8, one_part, 0)
        for chan in range(chans):
            shift = shifts_ref[shot, chan]
            whole_rows, part = shift // LANES, shift % LANES
            inside = (first_shot + shot >= low_ref[chan]) & (first_shot + shot < high_ref[chan])
            first = held[chan, pl.ds(lead - whole_rows, rows), :]
            second = held[chan, pl.ds(lead - 1 - whole_rows, rows), :]
            mixed = jnp.where(lane < LANES - part, first, second)
            moved = pltpu.roll(mixed, part, 1)
            out_ref[chan // 2, shot, chan % 2] = jnp.where(inside, moved, 0.0)
        return carry

    lax.fori_loop(0, shots, one_shot, 0)


def clean(shifts, low, high, left, down, up, right, chans, groups):
    shots, _, rows, _ = down.shape
    return pl.pallas_call(
        functools.partial(clean_kernel, (shots, chans, rows)),
        out_shape=jax.ShapeDtypeStruct((groups, shots, chans // groups, rows, LANES), jnp.float32),
        in_specs=[whole(pltpu.SMEM)] * 3 + [whole()] * 4,
        out_specs=whole(),
        scratch_shapes=[pltpu.VMEM((chans, 8 + rows, LANES), jnp.float32)],
        name="clean",
    )(shifts, low, high, left, down, up, right)


def real_forward(x):
    n = len(x)
    if n == 1:
        return [(x[0], None)]
    if n == 2:
        return [(x[0] + x[1], None), (x[0] - x[1], None)]
    even, odd = real_forward(x[0::2]), real_forward(x[1::2])
    out = [None] * (n // 2 + 1)
    for k in range(n // 4 + 1):
        (er, ei), (or_, oi) = even[k], odd[k]
        if k == 0:
            out[0] = (er + or_, None)
            out[n // 2] = (er - or_, None)
        elif 4 * k == n:
            out[k] = (er, -or_)
        else:
            c, s = math_cos(k, n), math_sin(k, n)
            tr, ti = or_ * c + oi * s, oi * c - or_ * s
            out[k] = (er + tr, ei + ti)
            out[n // 2 - k] = (er - tr, ti - ei)
    return out


def real_backward(spectrum, n):
    if n == 1:
        return [spectrum[0][0]]
    if n == 2:
        return [spectrum[0][0] + spectrum[1][0], spectrum[0][0] - spectrum[1][0]]
    even, odd = [None] * (n // 4 + 1), [None] * (n // 4 + 1)
    for k in range(n // 4 + 1):
        (ar, ai), (br, bi) = spectrum[k], spectrum[n // 2 - k]
        if k == 0:
            even[0], odd[0] = (ar + br, None), (ar - br, None)
        elif 4 * k == n:
            even[k], odd[k] = (ar + ar, None), (-(ai + ai), None)
        else:
            c, s = math_cos(k, n), math_sin(k, n)
            even[k] = (ar + br, ai - bi)
            dr, di = ar - br, ai + bi
            odd[k] = (dr * c - di * s, di * c + dr * s)
    first, second = real_backward(even, n // 2), real_backward(odd, n // 2)
    return [v for both in zip(first, second) for v in both]


def math_cos(k, n):
    return float(np.float32(np.cos(2 * np.pi * k / n)))


def math_sin(k, n):
    return float(np.float32(np.sin(2 * np.pi * k / n)))


def tables(shots, rows):
    a = np.arange(rows)
    outer = 2 * np.pi * (np.outer(a, a) % rows) / rows
    b = np.arange(LANES)
    inner = 2 * np.pi * (np.outer(b, b) % LANES) / LANES
    turn = 2 * np.pi * np.outer(a, b) / (rows * LANES)
    c, s = np.cos(outer), np.sin(outer)
    outer_forward = np.block([[c, s], [-s, c]])
    outer_backward = np.block([[c, -s], [s, c]])
    c, s = np.cos(inner), np.sin(inner)
    inner_forward = np.block([[c, -s], [s, c]])
    inner_backward = np.block([[c, s], [-s, c]]) / (shots * rows * LANES)
    twist = np.stack([np.cos(turn), np.sin(turn)])
    return [jnp.asarray(t, jnp.float32) for t in (outer_forward, outer_backward, inner_forward, inner_backward, twist)]


def dip_kernel(dims, bands_ref, data_ref, outer_f, outer_b, inner_f, inner_b, twist_ref, out_ref, held):
    shots, recs, rows = dims
    high = shots // 2
    first_rec = lax.axis_index("shot") * recs
    lane = lax.broadcasted_iota(jnp.int32, (rows, LANES), 1)
    frequency = lax.broadcasted_iota(jnp.int32, (rows, LANES), 0) + rows * lane
    distance = jnp.minimum(frequency, rows * LANES - frequency)

    for rec in range(recs):
        lanes = pl.ds(rec * LANES, LANES)

        def shots_forward(part, carry):
            place = pl.ds(pl.multiple_of(part * 8, 8), 8)
            below = pl.ds(pl.multiple_of(rows + part * 8, 8), 8)
            out = real_forward([data_ref[shot, rec, place, :] for shot in range(shots)])
            for k in range(high + 1):
                re, im = out[k]
                held[k, place, lanes] = re
                if k > 0:
                    held[k, below, lanes] = jnp.zeros_like(re) if im is None else im
            return carry

        lax.fori_loop(0, rows // 8, shots_forward, 0)

    def one_wave(k, carry):
        spec = jnp.dot(outer_f[...], held[k], precision=HIGHEST, preferred_element_type=jnp.float32)
        cos, sin = twist_ref[0], twist_ref[1]
        lines = []
        for rec in range(recs):
            re, im = spec[:rows, rec * LANES : (rec + 1) * LANES], spec[rows:, rec * LANES : (rec + 1) * LANES]
            lines.append(jnp.concatenate([re * cos + im * sin, im * cos - re * sin], axis=1))
        wave = jnp.concatenate(lines, axis=0)
        wave = jnp.dot(wave, inner_f[...], precision=HIGHEST, preferred_element_type=jnp.float32)
        keep = [distance >= k * bands_ref[first_rec + rec] for rec in range(recs)]
        keep = jnp.concatenate([jnp.concatenate([one, one], axis=1) for one in keep], axis=0)
        wave = jnp.where(keep, wave, 0.0)
        wave = jnp.dot(wave, inner_b[...], precision=HIGHEST, preferred_element_type=jnp.float32)
        res, ims = [], []
        for rec in range(recs):
            re, im = wave[rec * rows : (rec + 1) * rows, :LANES], wave[rec * rows : (rec + 1) * rows, LANES:]
            res.append(re * cos - im * sin)
            ims.append(im * cos + re * sin)
        back = jnp.concatenate([jnp.concatenate(res, axis=1), jnp.concatenate(ims, axis=1)], axis=0)
        held[k] = jnp.dot(outer_b[...], back, precision=HIGHEST, preferred_element_type=jnp.float32)
        return carry

    lax.fori_loop(1, high + 1, one_wave, 0)

    for rec in range(recs):
        lanes = pl.ds(rec * LANES, LANES)

        def shots_backward(part, carry):
            place = pl.ds(pl.multiple_of(part * 8, 8), 8)
            below = pl.ds(pl.multiple_of(rows + part * 8, 8), 8)
            spectrum = [(held[0, place, lanes] * (1.0 / shots), None)]
            for k in range(1, high + 1):
                spectrum.append((held[k, place, lanes], held[k, below, lanes] if k < high else None))
            back = real_backward(spectrum, shots)
            for shot in range(shots):
                out_ref[shot, pl.ds(part * (8 * recs) + rec, 8, stride=recs), :] = back[shot]
            return carry

        lax.fori_loop(0, rows // 8, shots_backward, 0)


def dip_filter(gathered, dip_band):
    shots, recs, rows, _ = gathered.shape
    out = pl.pallas_call(
        functools.partial(dip_kernel, (shots, recs, rows)),
        out_shape=jax.ShapeDtypeStruct((shots, rows * recs, LANES), jnp.float32),
        in_specs=[whole(pltpu.SMEM)] + [whole()] * 6,
        out_specs=whole(),
        scratch_shapes=[pltpu.VMEM((shots // 2 + 1, 2 * rows, recs * LANES), jnp.float32)],
        name="dip",
    )(dip_band, gathered, *tables(shots, rows))
    return out.reshape(shots, rows, recs, LANES).transpose(0, 2, 1, 3).reshape(shots, recs, rows * LANES)


def local(traces, shifts, aperture_lo, aperture_hi, dip_band):
    shots, chans, length = traces.shape
    blocks, groups = lax.axis_size("chan"), lax.axis_size("shot")
    down, up = align(traces, shifts)
    left = lax.ppermute(up, "chan", [(i, i + 1) for i in range(blocks - 1)])
    right = lax.ppermute(down, "chan", [(i + 1, i) for i in range(blocks - 1)])
    parted = clean(shifts, aperture_lo, aperture_hi, left, down, up, right, chans, groups)
    arrived = lax.all_to_all(parted, "shot", split_axis=0, concat_axis=0, tiled=True)
    gathered = arrived.reshape(groups * shots, chans // groups, length // LANES, LANES)
    return dip_filter(gathered, dip_band)


def solution(mesh):
    return jax.shard_map(
        local,
        mesh=mesh,
        in_specs=(P("shot", "chan", None), P("shot", "chan"), P("chan"), P("chan"), P("chan")),
        out_specs=P(None, ("chan", "shot"), None),
        check_vma=False,
    )
```

profile of v0, /device:TPU:24, one launch (start us, length us, event | category | flops | bytes accessed | tf_op | source)
XLA Modules:
  0.0 77.8 jit_solution(9272466881576628547)
XLA Ops:
  0.0 3.6 %align.1 = (f32[4,10,32,128]{3,2,1,0:T(8,128)}, f32[4,10,32,128]{3,2,1,0:T(8,128)}) custom-call(s32[4,16]{1,0:T(4,128)} %shifts_ref.3, f32[2048,128]{1,0:T(8,128)} %bitcast.12), custom_call_target="tpu_custom_call" | custom-call | tf_op jit(solution)/shard_map/align/pallas_call | solution.py:59
  3.6 3.8 %collective-permute-start = (f32[4,10,32,128]{3,2,1,0:T(8,128)}, f32[4,10,32,128]{3,2,1,0:T(8,128)S(1)}, u32[]{:S(2)}, u32[]{:S(2)}) collective-permute-start(f32[4,10,32,128]{3,2,1,0:T(8,128)} %get-tuple-element.7.up_ref), channel_id=1, source_target_pairs={{0,1},{1,2},{2,3},{3,4},{4,5},{5,6},{6,7},{7,8},{8,9},{9,10},{10,1... | collective-permute-start | bytes 1966088 | tf_op jit(solution)/shard_map/ppermute | solution.py:326
  7.4 9.7 %collective-permute-start.1 = (f32[4,10,32,128]{3,2,1,0:T(8,128)}, f32[4,10,32,128]{3,2,1,0:T(8,128)S(1)}, u32[]{:S(2)}, u32[]{:S(2)}) collective-permute-start(f32[4,10,32,128]{3,2,1,0:T(8,128)} %get-tuple-element.8.down_ref), channel_id=1, source_target_pairs={{1,0},{2,1},{3,2},{4,3},{5,4},{6,5},{7,6},{8,7},{9,8},{10,9},{11,1... | collective-permute-start | bytes 1966088 | tf_op jit(solution)/shard_map/ppermute | solution.py:327
  17.1 13.0 %collective-permute-done.left_ref = f32[4,10,32,128]{3,2,1,0:T(8,128)S(1)} collective-permute-done((f32[4,10,32,128]{3,2,1,0:T(8,128)}, f32[4,10,32,128]{3,2,1,0:T(8,128)S(1)}, u32[]{:S(2)}, u32[]{:S(2)}) %collective-permute-start) | collective-permute-done | bytes 655392 | tf_op jit(solution)/shard_map/ppermute | solution.py:326
  30.1 0.0 copy-start
  30.1 1.3 %collective-permute-done.1.right_ref = f32[4,10,32,128]{3,2,1,0:T(8,128)S(1)} collective-permute-done((f32[4,10,32,128]{3,2,1,0:T(8,128)}, f32[4,10,32,128]{3,2,1,0:T(8,128)S(1)}, u32[]{:S(2)}, u32[]{:S(2)}) %collective-permute-start.1) | collective-permute-done | bytes 655392 | tf_op jit(solution)/shard_map/ppermute | solution.py:327
  31.4 0.0 copy-done
  31.4 0.0 copy-start.1
  31.4 0.8 %copy-done.1 = f32[4,10,32,128]{3,2,1,0:T(8,128)} copy-done((f32[4,10,32,128]{3,2,1,0:T(8,128)}, f32[4,10,32,128]{3,2,1,0:T(8,128)S(1)}, u32[]{:S(2)}) %copy-start.1) | copy-done | bytes 655384
  32.2 5.0 %clean.1 = f32[8,4,2,32,128]{4,3,2,1,0:T(8,128)} custom-call(s32[4,16]{1,0:T(4,128)} %shifts_ref.3, s32[16]{0:T(128)} %low_ref.1, s32[16]{0:T(128)} %high_ref.1, f32[4,10,32,128]{3,2,1,0:T(8,128)} %copy-done, f32[4,10,32,128]{3,2,1,0:T(8,128)} %get-tuple-element.8.down_ref, f32[4,10,32,128]{3,2,1,0:T(8,128)} %get-tuple-element.7.up_ref, ...), custom_call_target="tpu_custom_call" | custom-call | tf_op jit(solution)/shard_map/clean/pallas_call | solution.py:166
  37.2 20.4 %all_to_all.5 = f32[8,4,2,32,128]{4,3,2,1,0:T(8,128)} all-to-all(f32[8,4,2,32,128]{4,3,2,1,0:T(8,128)} %clean.1), channel_id=1, replica_groups=mesh['shot'=8,'chan'=64] {'shot'}, dimensions={0} | all-to-all | bytes 2097152 | tf_op jit(solution)/shard_map/all_to_all | solution.py:329
  57.6 20.2 %dip.1 = f32[32,64,128]{2,1,0:T(8,128)} custom-call(s32[16]{0:T(128)} %bands_ref.1, f32[32,2,32,128]{3,2,1,0:T(8,128)} %bitcast.11, f32[64,64]{1,0:T(8,128)} %constant.10.clone.outer_f, f32[64,64]{1,0:T(8,128)} %constant.11.clone.outer_b, f32[256,256]{1,0:T(8,128)} %constant.12.clone.inner_f, f32[256,256]{1,0:T(8,128)} %constant.13.clone.inner_b, ...), custom_call_target="tpu_custom_call" | custom-call | tf_op jit(solution)/shard_map/dip/pallas_call | solution.py:311
Async XLA Ops:
  3.6 26.5 %collective-permute-start = (f32[4,10,32,128]{3,2,1,0:T(8,128)}, f32[4,10,32,128]{3,2,1,0:T(8,128)S(1)}, u32[]{:S(2)}, u32[]{:S(2)}) collective-permute-start(f32[4,10,32,128]{3,2,1,0:T(8,128)} %get-tuple-element.7.up_ref), channel_id=1, source_target_pairs={{0,1},{1,2},{2,3},{3,4},{4,5},{5,6},{6,7},{7,8},{8,9},{9,10},{10,1... | collective-permute-start | bytes 1966088 | tf_op jit(solution)/shard_map/ppermute | solution.py:326
  7.4 24.0 %collective-permute-start.1 = (f32[4,10,32,128]{3,2,1,0:T(8,128)}, f32[4,10,32,128]{3,2,1,0:T(8,128)S(1)}, u32[]{:S(2)}, u32[]{:S(2)}) collective-permute-start(f32[4,10,32,128]{3,2,1,0:T(8,128)} %get-tuple-element.8.down_ref), channel_id=1, source_target_pairs={{1,0},{2,1},{3,2},{4,3},{5,4},{6,5},{7,6},{8,7},{9,8},{10,9},{11,1... | collective-permute-start | bytes 1966088 | tf_op jit(solution)/shard_map/ppermute | solution.py:327
  30.1 1.3 %copy-start = (f32[4,10,32,128]{3,2,1,0:T(8,128)}, f32[4,10,32,128]{3,2,1,0:T(8,128)S(1)}, u32[]{:S(2)}) copy-start(f32[4,10,32,128]{3,2,1,0:T(8,128)S(1)} %collective-permute-done.left_ref) | copy-start | bytes 1966084
  31.4 0.8 %copy-start.1 = (f32[4,10,32,128]{3,2,1,0:T(8,128)}, f32[4,10,32,128]{3,2,1,0:T(8,128)S(1)}, u32[]{:S(2)}) copy-start(f32[4,10,32,128]{3,2,1,0:T(8,128)S(1)} %collective-permute-done.1.right_ref) | copy-start | bytes 1966084
where the time goes:
time: 78.1 us; the launch traced here: 77.8 us
  Pallas kernels  28.8 us (37%)
  blocking collectives  20.4 us (26%)
  waiting for transfers between devices  14.3 us (18%)
  starting transfers between devices  13.5 us (17%)
  local copies, waits for them, and re-layouts  0.84 us (1%)
    all_to_all x1, blocking collectives, local(): lax.all_to_all(parted, 'shot', split_axis=0, concat_axis=0, tiled=True)  20.4 us
    pallas_call x1, Pallas kernels, dip_filter(): pl.pallas_call(functools.partial(dip_kernel, (shots, recs, rows)), out_sh...  20.2 us
    ppermute x1, waiting for transfers between devices, local(): left = lax.ppermute(up, 'chan', [(i, i + 1) for i in range(blocks - 1)])  13 us
    ppermute x1, starting transfers between devices, local(): right = lax.ppermute(down, 'chan', [(i + 1, i) for i in range(blocks - 1)])  9.68 us
    pallas_call x1, Pallas kernels, clean(): pl.pallas_call(functools.partial(clean_kernel, (shots, chans, rows)), out...  4.96 us
    ppermute x1, starting transfers between devices, local(): left = lax.ppermute(up, 'chan', [(i, i + 1) for i in range(blocks - 1)])  3.83 us
    pallas_call x1, Pallas kernels, align(): pl.pallas_call(functools.partial(align_kernel, (shots, chans, rows)), out...  3.6 us
  transfers between devices with their start and end apart: 2, of which 2 were waited for; matrix products, arithmetic and copies ran while one was open for 0% of the time, Pallas kernels for 0%

commit v1 on v0

--- a/solution.py
+++ b/solution.py
@@ -11,7 +11,8 @@
 LANES = 128
 HALF = 5
 HALO = 2 * HALF
-HIGHEST = lax.Precision.HIGHEST
+GRANT = 16 << 20
+WAVES = 4
 
 
 def whole(space=pltpu.VMEM):
@@ -65,6 +66,7 @@
             pltpu.VMEM((shots * chans * rows + pad, LANES), jnp.float32),
             pltpu.SemaphoreType.DMA((shots,)),
         ],
+        compiler_params=pltpu.CompilerParams(vmem_limit_bytes=GRANT),
         name="align",
     )(shifts, flat)
 
@@ -169,6 +171,7 @@
         in_specs=[whole(pltpu.SMEM)] * 3 + [whole()] * 4,
         out_specs=whole(),
         scratch_shapes=[pltpu.VMEM((chans, 8 + rows, LANES), jnp.float32)],
+        compiler_params=pltpu.CompilerParams(vmem_limit_bytes=GRANT),
         name="clean",
     )(shifts, low, high, left, down, up, right)
 
@@ -225,6 +228,17 @@
     return float(np.float32(np.sin(2 * np.pi * k / n)))
 
 
+def split(x):
+    top = x.astype(jnp.bfloat16)
+    return top, (x - top.astype(jnp.float32)).astype(jnp.bfloat16)
+
+
+def constant_split(x):
+    x = np.asarray(x, np.float32)
+    top = x.astype(jnp.bfloat16)
+    return top, (x - top.astype(np.float32)).astype(jnp.bfloat16)
+
+
 def tables(shots, rows):
     a = np.arange(rows)
     outer = 2 * np.pi * (np.outer(a, a) % rows) / rows
@@ -237,8 +251,20 @@
     c, s = np.cos(inner), np.sin(inner)
     inner_forward = np.block([[c, -s], [s, c]])
     inner_backward = np.block([[c, s], [-s, c]]) / (shots * rows * LANES)
-    twist = np.stack([np.cos(turn), np.sin(turn)])
-    return [jnp.asarray(t, jnp.float32) for t in (outer_forward, outer_backward, inner_forward, inner_backward, twist)]
+    left = []
+    for matrix in (outer_forward, outer_backward):
+        top, rest = constant_split(matrix)
+        left.append(jnp.asarray(np.concatenate([top, top, rest], axis=1)))
+    right = []
+    for matrix in (inner_forward, inner_backward):
+        top, rest = constant_split(matrix)
+        right.append(jnp.asarray(np.concatenate([top, top, rest], axis=0)))
+    twist = jnp.asarray(np.stack([np.cos(turn), np.sin(turn)]), jnp.float32)
+    return (*left, *right, twist)
+
+
+def dot(a, b):
+    return jnp.dot(a, b, preferred_element_type=jnp.float32)
 
 
 def dip_kernel(dims, bands_ref, data_ref, outer_f, outer_b, inner_f, inner_b, twist_ref, out_ref, held):
@@ -265,29 +291,52 @@
 
         lax.fori_loop(0, rows // 8, shots_forward, 0)
 
-    def one_wave(k, carry):
-        spec = jnp.dot(outer_f[...], held[k], precision=HIGHEST, preferred_element_type=jnp.float32)
+    def left_product(matrix, k):
+        top, rest = split(held[k])
+        return dot(matrix[...], jnp.concatenate([top, rest, top], axis=0))
+
+    def right_product(lines, matrix):
+        top, rest = split(lines)
+        return dot(jnp.concatenate([top, rest, top], axis=1), matrix[...])
+
+    def some_waves(step, carry):
         cos, sin = twist_ref[0], twist_ref[1]
+        first = 1 + step * WAVES
         lines = []
-        for rec in range(recs):
-            re, im = spec[:rows, rec * LANES : (rec + 1) * LANES], spec[rows:, rec * LANES : (rec + 1) * LANES]
-            lines.append(jnp.concatenate([re * cos + im * sin, im * cos - re * sin], axis=1))
-        wave = jnp.concatenate(lines, axis=0)
-        wave = jnp.dot(wave, inner_f[...], precision=HIGHEST, preferred_element_type=jnp.float32)
-        keep = [distance >= k * bands_ref[first_rec + rec] for rec in range(recs)]
-        keep = jnp.concatenate([jnp.concatenate([one, one], axis=1) for one in keep], axis=0)
-        wave = jnp.where(keep, wave, 0.0)
-        wave = jnp.dot(wave, inner_b[...], precision=HIGHEST, preferred_element_type=jnp.float32)
-        res, ims = [], []
-        for rec in range(recs):
-            re, im = wave[rec * rows : (rec + 1) * rows, :LANES], wave[rec * rows : (rec + 1) * rows, LANES:]
-            res.append(re * cos - im * sin)
-            ims.append(im * cos + re * sin)
-        back = jnp.concatenate([jnp.concatenate(res, axis=1), jnp.concatenate(ims, axis=1)], axis=0)
-        held[k] = jnp.dot(outer_b[...], back, precision=HIGHEST, preferred_element_type=jnp.float32)
+        for i in range(WAVES):
+            spec = left_product(outer_f, first + i)
+            for rec in range(recs):
+                mine = slice(rec * LANES, (rec + 1) * LANES)
+                re, im = spec[:rows, mine], spec[rows:, mine]
+                lines.append(jnp.concatenate([re * cos + im * sin, im * cos - re * sin], axis=1))
+        wave = right_product(jnp.concatenate(lines, axis=0), inner_f)
+        kept = []
+        for i in range(WAVES):
+            for rec in range(recs):
+                n = (i * recs + rec) * rows
+                keep = distance >= (first + i) * bands_ref[first_rec + rec]
+                kept.append(
+                    jnp.concatenate(
+                        [
+                            jnp.where(keep, wave[n : n + rows, :LANES], 0.0),
+                            jnp.where(keep, wave[n : n + rows, LANES:], 0.0),
+                        ],
+                        axis=1,
+                    )
+                )
+        wave = right_product(jnp.concatenate(kept, axis=0), inner_b)
+        for i in range(WAVES):
+            for rec in range(recs):
+                n = (i * recs + rec) * rows
+                lanes = slice(rec * LANES, (rec + 1) * LANES)
+                re, im = wave[n : n + rows, :LANES], wave[n : n + rows, LANES:]
+                held[first + i, :rows, lanes] = re * cos - im * sin
+                held[first + i, rows:, lanes] = im * cos + re * sin
+        for i in range(WAVES):
+            held[first + i] = left_product(outer_b, first + i)
         return carry
 
-    lax.fori_loop(1, high + 1, one_wave, 0)
+    lax.fori_loop(0, high // WAVES, some_waves, 0)
 
     for rec in range(recs):
         lanes = pl.ds(rec * LANES, LANES)
@@ -314,6 +363,7 @@
         in_specs=[whole(pltpu.SMEM)] + [whole()] * 6,
         out_specs=whole(),
         scratch_shapes=[pltpu.VMEM((shots // 2 + 1, 2 * rows, recs * LANES), jnp.float32)],
+        compiler_params=pltpu.CompilerParams(vmem_limit_bytes=GRANT),
         name="dip",
     )(dip_band, gathered, *tables(shots, rows))
     return out.reshape(shots, rows, recs, LANES).transpose(0, 2, 1, 3).reshape(shots, recs, rows * LANES)

time: 78.1 us -> 60.8 us (0.78)
  Pallas kernels: 28.8 us -> 10.2 us
  local copies, waits for them, and re-layouts: 0.84 us -> 2.57 us
    pallas_call x1, Pallas kernels: 20.2 us -> 5.97 us  [dip_filter(): pl.pallas_call(functools.partial(dip_kernel, (shots, recs, rows)), out_sh...]
    pallas_call x1, Pallas kernels: 3.6 us -> 1.37 us  [align(): pl.pallas_call(functools.partial(align_kernel, (shots, chans, rows)), out...]
    pallas_call x1, Pallas kernels: 4.96 us -> 2.88 us  [clean(): pl.pallas_call(functools.partial(clean_kernel, (shots, chans, rows)), out...]
    unnamed x4 -> x20, local copies, waits for them, and re-layouts: 0.84 us -> 2.57 us
where the time goes in v1:
time: 60.8 us; the launch traced here: 60.6 us
  blocking collectives  20.2 us (33%)
  waiting for transfers between devices  14 us (23%)
  starting transfers between devices  13.5 us (22%)
  Pallas kernels  10.2 us (17%)
  local copies, waits for them, and re-layouts  2.57 us (4%)
    all_to_all x1, blocking collectives, local(): lax.all_to_all(parted, 'shot', split_axis=0, concat_axis=0, tiled=True)  20.2 us
    ppermute x1, waiting for transfers between devices, local(): left = lax.ppermute(up, 'chan', [(i, i + 1) for i in range(blocks - 1)])  12.8 us
    ppermute x1, starting transfers between devices, local(): right = lax.ppermute(down, 'chan', [(i + 1, i) for i in range(blocks - 1)])  9.68 us
    pallas_call x1, Pallas kernels, dip_filter(): pl.pallas_call(functools.partial(dip_kernel, (shots, recs, rows)), out_sh...  5.97 us
    ppermute x1, starting transfers between devices, local(): left = lax.ppermute(up, 'chan', [(i, i + 1) for i in range(blocks - 1)])  3.83 us
    pallas_call x1, Pallas kernels, clean(): pl.pallas_call(functools.partial(clean_kernel, (shots, chans, rows)), out...  2.88 us
    unnamed x20, local copies, waits for them, and re-layouts  2.57 us
    pallas_call x1, Pallas kernels, align(): pl.pallas_call(functools.partial(align_kernel, (shots, chans, rows)), out...  1.37 us
  transfers between devices with their start and end apart: 2, of which 2 were waited for; matrix products, arithmetic and copies ran while one was open for 0% of the time, Pallas kernels for 0%

profile of v1, /device:TPU:24, one launch (start us, length us, event | category | flops | bytes accessed | tf_op | source)
XLA Modules:
  0.0 60.6 jit_solution(2350474672400598221)
XLA Ops:
  0.0 1.2 %copy-done = f32[4,16,4096]{2,1,0:T(8,128)S(1)} copy-done((f32[4,16,4096]{2,1,0:T(8,128)S(1)}, f32[4,16,4096]{2,1,0:T(8,128)}, u32[]{:S(2)}) %copy-start) | copy-done | bytes 1048600
  1.2 0.7 %copy-done.6 = s32[4,16]{1,0:T(4,128)S(1)} copy-done((s32[4,16]{1,0:T(4,128)S(1)}, s32[4,16]{1,0:T(4,128)}, u32[]{:S(2)}) %copy-start.6) | copy-done | bytes 280
  1.9 1.4 %align.1 = (f32[4,10,32,128]{3,2,1,0:T(8,128)S(1)}, f32[4,10,32,128]{3,2,1,0:T(8,128)S(1)}) custom-call(s32[4,16]{1,0:T(4,128)S(1)} %copy-done.6, f32[2048,128]{1,0:T(8,128)S(1)} %bitcast.12), custom_call_target="tpu_custom_call" | custom-call | tf_op jit(solution)/shard_map/align/pallas_call | solution.py:60
  3.3 0.0 copy-start.8
  3.3 0.0 copy-start.9
  3.3 3.8 %collective-permute-start = (f32[4,10,32,128]{3,2,1,0:T(8,128)S(1)}, f32[4,10,32,128]{3,2,1,0:T(8,128)S(1)}, u32[]{:S(2)}, u32[]{:S(2)}) collective-permute-start(f32[4,10,32,128]{3,2,1,0:T(8,128)S(1)} %get-tuple-element.7.up_ref), channel_id=1, source_target_pairs={{0,1},{1,2},{2,3},{3,4},{4,5},{5,6},{6,7},{7,8},{8,9},{9,10},{10,1... | collective-permute-start | bytes 1966088 | tf_op jit(solution)/shard_map/ppermute | solution.py:376
  7.1 9.7 %collective-permute-start.1 = (f32[4,10,32,128]{3,2,1,0:T(8,128)S(1)}, f32[4,10,32,128]{3,2,1,0:T(8,128)S(1)}, u32[]{:S(2)}, u32[]{:S(2)}) collective-permute-start(f32[4,10,32,128]{3,2,1,0:T(8,128)S(1)} %get-tuple-element.8.down_ref), channel_id=1, source_target_pairs={{1,0},{2,1},{3,2},{4,3},{5,4},{6,5},{7,6},{8,7},{9,8},{10,9},{11,1... | collective-permute-start | bytes 1966088 | tf_op jit(solution)/shard_map/ppermute | solution.py:377
  16.8 12.8 %collective-permute-done.left_ref = f32[4,10,32,128]{3,2,1,0:T(8,128)S(1)} collective-permute-done((f32[4,10,32,128]{3,2,1,0:T(8,128)S(1)}, f32[4,10,32,128]{3,2,1,0:T(8,128)S(1)}, u32[]{:S(2)}, u32[]{:S(2)}) %collective-permute-start) | collective-permute-done | bytes 655392 | tf_op jit(solution)/shard_map/ppermute | solution.py:376
  29.6 1.2 %collective-permute-done.1.right_ref = f32[4,10,32,128]{3,2,1,0:T(8,128)S(1)} collective-permute-done((f32[4,10,32,128]{3,2,1,0:T(8,128)S(1)}, f32[4,10,32,128]{3,2,1,0:T(8,128)S(1)}, u32[]{:S(2)}, u32[]{:S(2)}) %collective-permute-start.1) | collective-permute-done | bytes 655392 | tf_op jit(solution)/shard_map/ppermute | solution.py:377
  30.8 0.0 copy-done.8
  30.8 0.0 copy-done.9
  30.8 2.9 %clean.1 = f32[8,4,2,32,128]{4,3,2,1,0:T(8,128)S(1)} custom-call(s32[4,16]{1,0:T(4,128)S(1)} %copy-done.6, s32[16]{0:T(128)S(1)} %copy-done.8, s32[16]{0:T(128)S(1)} %copy-done.9, f32[4,10,32,128]{3,2,1,0:T(8,128)S(1)} %collective-permute-done.left_ref, f32[4,10,32,128]{3,2,1,0:T(8,128)S(1)} %get-tuple-element.8.down_ref, ...), custom_call_target="tpu_custom_call" | custom-call | tf_op jit(solution)/shard_map/clean/pallas_call | solution.py:168
  33.7 0.0 copy-start.2
  33.7 0.0 copy-start.3
  33.7 0.0 copy-start.4
  33.7 0.0 copy-start.5
  33.7 20.2 %all_to_all.5 = f32[8,4,2,32,128]{4,3,2,1,0:T(8,128)S(1)} all-to-all(f32[8,4,2,32,128]{4,3,2,1,0:T(8,128)S(1)} %clean.1), channel_id=1, replica_groups=mesh['shot'=8,'chan'=64] {'shot'}, dimensions={0} | all-to-all | bytes 2097152 | tf_op jit(solution)/shard_map/all_to_all | solution.py:379
  53.9 0.0 copy-done.1
  54.0 0.0 copy-done.2
  54.0 0.0 copy-done.3
  54.0 0.0 copy-done.4
  54.0 0.0 copy-done.5
  54.0 0.6 %copy-done.7 = s32[16]{0:T(128)S(1)} copy-done((s32[16]{0:T(128)S(1)}, s32[16]{0:T(128)}, u32[]{:S(2)}) %copy-start.7) | copy-done | bytes 88
  54.6 6.0 %dip.1 = f32[32,64,128]{2,1,0:T(8,128)} custom-call(s32[16]{0:T(128)S(1)} %copy-done.7, f32[32,2,32,128]{3,2,1,0:T(8,128)S(1)} %bitcast.11, bf16[64,192]{1,0:T(8,128)(2,1)S(1)} %copy-done.5, bf16[64,192]{1,0:T(8,128)(2,1)S(1)} %copy-done.4, bf16[768,256]{1,0:T(8,128)(2,1)S(1)} %copy-done.2, bf16[768,256]{1,0:T(8,128)(2,1)S(1)} %copy-done.1, ...), custom_call_target="tpu_custom_call" | custom-call | tf_op jit(solution)/shard_map/dip/pallas_call | solution.py:360
  (4 shorter events, 0.0 us)
Async XLA Ops:
  0.0 1.2 %copy-start = (f32[4,16,4096]{2,1,0:T(8,128)S(1)}, f32[4,16,4096]{2,1,0:T(8,128)}, u32[]{:S(2)}) copy-start(f32[4,16,4096]{2,1,0:T(8,128)} %param.10) | copy-start | bytes 3145732
  1.2 0.7 %copy-start.6 = (s32[4,16]{1,0:T(4,128)S(1)}, s32[4,16]{1,0:T(4,128)}, u32[]{:S(2)}) copy-start(s32[4,16]{1,0:T(4,128)} %shifts_ref.3) | copy-start | bytes 772
  3.3 27.5 %copy-start.8 = (s32[16]{0:T(128)S(1)}, s32[16]{0:T(128)}, u32[]{:S(2)}) copy-start(s32[16]{0:T(128)} %low_ref.1) | copy-start | bytes 196
  3.3 27.5 %copy-start.9 = (s32[16]{0:T(128)S(1)}, s32[16]{0:T(128)}, u32[]{:S(2)}) copy-start(s32[16]{0:T(128)} %high_ref.1) | copy-start | bytes 196
  3.3 26.3 %collective-permute-start = (f32[4,10,32,128]{3,2,1,0:T(8,128)S(1)}, f32[4,10,32,128]{3,2,1,0:T(8,128)S(1)}, u32[]{:S(2)}, u32[]{:S(2)}) collective-permute-start(f32[4,10,32,128]{3,2,1,0:T(8,128)S(1)} %get-tuple-element.7.up_ref), channel_id=1, source_target_pairs={{0,1},{1,2},{2,3},{3,4},{4,5},{5,6},{6,7},{7,8},{8,9},{9,10},{10,1... | collective-permute-start | bytes 1966088 | tf_op jit(solution)/shard_map/ppermute | solution.py:376
  7.1 23.7 %collective-permute-start.1 = (f32[4,10,32,128]{3,2,1,0:T(8,128)S(1)}, f32[4,10,32,128]{3,2,1,0:T(8,128)S(1)}, u32[]{:S(2)}, u32[]{:S(2)}) collective-permute-start(f32[4,10,32,128]{3,2,1,0:T(8,128)S(1)} %get-tuple-element.8.down_ref), channel_id=1, source_target_pairs={{1,0},{2,1},{3,2},{4,3},{5,4},{6,5},{7,6},{8,7},{9,8},{10,9},{11,1... | collective-permute-start | bytes 1966088 | tf_op jit(solution)/shard_map/ppermute | solution.py:377
  33.7 20.3 %copy-start.1 = (bf16[768,256]{1,0:T(8,128)(2,1)S(1)}, bf16[768,256]{1,0:T(8,128)(2,1)}, u32[]{:S(2)}) copy-start(bf16[768,256]{1,0:T(8,128)(2,1)} %constant.13.clone.inner_b) | copy-start | bytes 1179652
  33.7 20.3 %copy-start.2 = (bf16[768,256]{1,0:T(8,128)(2,1)S(1)}, bf16[768,256]{1,0:T(8,128)(2,1)}, u32[]{:S(2)}) copy-start(bf16[768,256]{1,0:T(8,128)(2,1)} %constant.12.clone.inner_f) | copy-start | bytes 1179652
  33.7 20.3 %copy-start.3 = (f32[2,32,128]{2,1,0:T(8,128)S(1)}, f32[2,32,128]{2,1,0:T(8,128)}, u32[]{:S(2)}) copy-start(f32[2,32,128]{2,1,0:T(8,128)} %constant.14.clone.twist_ref) | copy-start | bytes 98308
  33.7 20.2 %copy-start.4 = (bf16[64,192]{1,0:T(8,128)(2,1)S(1)}, bf16[64,192]{1,0:T(8,128)(2,1)}, u32[]{:S(2)}) copy-start(bf16[64,192]{1,0:T(8,128)(2,1)} %constant.11.clone.outer_b) | copy-start | bytes 73732
  33.7 20.2 %copy-start.5 = (bf16[64,192]{1,0:T(8,128)(2,1)S(1)}, bf16[64,192]{1,0:T(8,128)(2,1)}, u32[]{:S(2)}) copy-start(bf16[64,192]{1,0:T(8,128)(2,1)} %constant.10.clone.outer_f) | copy-start | bytes 73732
  53.9 0.7 %copy-start.7 = (s32[16]{0:T(128)S(1)}, s32[16]{0:T(128)}, u32[]{:S(2)}) copy-start(s32[16]{0:T(128)} %bands_ref.1) | copy-start | bytes 196

commit v2 on v1

--- a/solution.py
+++ b/solution.py
@@ -11,39 +11,39 @@
 LANES = 128
 HALF = 5
 HALO = 2 * HALF
+TAIL = 8 * 9
 GRANT = 16 << 20
-WAVES = 4
+WAVES = 16
 
 
 def whole(space=pltpu.VMEM):
     return pl.BlockSpec(memory_space=space)
 
 
-def align_kernel(dims, shifts_ref, traces_ref, down_ref, up_ref, held, sems):
+def align_kernel(dims, shifts_ref, traces_ref, down_ref, up_ref, held, shifts, shift_sem, sems):
     shots, chans, rows = dims
     tiles = chans * rows
+    count = pltpu.make_async_copy(shifts_ref, shifts, shift_sem)
+    count.start()
+    copies = []
     for shot in range(shots):
-        pltpu.make_async_copy(
-            traces_ref.at[pl.ds(shot * tiles, tiles)], held.at[pl.ds(shot * tiles, tiles)], sems.at[shot]
-        ).start()
-    held[pl.ds(shots * tiles, held.shape[0] - shots * tiles), :] = jnp.zeros(
-        (held.shape[0] - shots * tiles, LANES), jnp.float32
-    )
+        source, target = traces_ref.at[pl.ds(shot * tiles, tiles)], held.at[shot, pl.ds(0, tiles)]
+        copies.append(pltpu.make_async_copy(source, target, sems.at[shot]))
+        copies[-1].start()
+        held[shot, pl.ds(tiles, TAIL), :] = jnp.zeros((TAIL, LANES), jnp.float32)
     lane = lax.broadcasted_iota(jnp.int32, (rows, LANES), 1)
     sample = lax.broadcasted_iota(jnp.int32, (rows, LANES), 0) * LANES + lane
+    count.wait()
     for shot in range(shots):
-        pltpu.make_async_copy(
-            traces_ref.at[pl.ds(shot * tiles, tiles)], held.at[pl.ds(shot * tiles, tiles)], sems.at[shot]
-        ).wait()
-    for shot in range(shots):
+        copies[shot].wait()
         for chan in range(chans):
-            shift = shifts_ref[shot, chan]
-            whole_rows, part = shift // LANES, shift % LANES
-            base = shot * tiles + (chan // 8) * (rows * 8) + chan % 8
-            first = held[pl.ds(base + whole_rows * 8, rows, stride=8), :]
-            second = held[pl.ds(base + whole_rows * 8 + 8, rows, stride=8), :]
+            shift = shifts[shot, chan]
+            part = shift & (LANES - 1)
+            base = (chan // 8) * (rows * 8) + chan % 8 + ((shift >> 7) << 3)
+            first = held[shot, pl.ds(base, rows, stride=8), :]
+            second = held[shot, pl.ds(base + 8, rows, stride=8), :]
             mixed = jnp.where(lane >= part, first, second)
-            moved = pltpu.roll(mixed, (LANES - part) % LANES, 1)
+            moved = pltpu.roll(mixed, (LANES - part) & (LANES - 1), 1)
             moved = jnp.where(sample < rows * LANES - shift, moved, 0.0)
             if chan < HALO:
                 down_ref[shot, chan] = moved
@@ -56,19 +56,20 @@
     rows = length // LANES
     flat = traces.reshape(shots, chans // 8, 8, rows, LANES).transpose(0, 1, 3, 2, 4).reshape(-1, LANES)
     edge = jax.ShapeDtypeStruct((shots, HALO, rows, LANES), jnp.float32)
-    pad = 8 * 9
     return pl.pallas_call(
         functools.partial(align_kernel, (shots, chans, rows)),
         out_shape=(edge, edge),
-        in_specs=[whole(pltpu.SMEM), whole(pl.ANY)],
+        in_specs=[whole(pltpu.HBM), whole(pltpu.HBM)],
         out_specs=(whole(), whole()),
         scratch_shapes=[
-            pltpu.VMEM((shots * chans * rows + pad, LANES), jnp.float32),
+            pltpu.VMEM((shots, chans * rows + TAIL, LANES), jnp.float32),
+            pltpu.SMEM((shots, chans), jnp.int32),
+            pltpu.SemaphoreType.DMA,
             pltpu.SemaphoreType.DMA((shots,)),
         ],
         compiler_params=pltpu.CompilerParams(vmem_limit_bytes=GRANT),
         name="align",
-    )(shifts, flat)
+    )(pltpu.with_memory_space_constraint(shifts, pltpu.HBM), pltpu.with_memory_space_constraint(flat, pltpu.HBM))
 
 
 def order(a, b):
@@ -151,7 +152,7 @@
         lax.fori_loop(0, rows // 8, one_part, 0)
         for chan in range(chans):
             shift = shifts_ref[shot, chan]
-            whole_rows, part = shift // LANES, shift % LANES
+            whole_rows, part = shift >> 7, shift & (LANES - 1)
             inside = (first_shot + shot >= low_ref[chan]) & (first_shot + shot < high_ref[chan])
             first = held[chan, pl.ds(lead - whole_rows, rows), :]
             second = held[chan, pl.ds(lead - 1 - whole_rows, rows), :]
@@ -267,29 +268,26 @@
     return jnp.dot(a, b, preferred_element_type=jnp.float32)
 
 
-def dip_kernel(dims, bands_ref, data_ref, outer_f, outer_b, inner_f, inner_b, twist_ref, out_ref, held):
+def dip_kernel(dims, bands_ref, data_ref, outer_f, outer_b, inner_f, inner_b, twist_ref, result_ref, held, out_ref, bands, band_sem, sems):
     shots, recs, rows = dims
     high = shots // 2
+    band_copy = pltpu.make_async_copy(bands_ref, bands, band_sem)
+    band_copy.start()
     first_rec = lax.axis_index("shot") * recs
     lane = lax.broadcasted_iota(jnp.int32, (rows, LANES), 1)
     frequency = lax.broadcasted_iota(jnp.int32, (rows, LANES), 0) + rows * lane
     distance = jnp.minimum(frequency, rows * LANES - frequency)
 
-    for rec in range(recs):
-        lanes = pl.ds(rec * LANES, LANES)
-
-        def shots_forward(part, carry):
-            place = pl.ds(pl.multiple_of(part * 8, 8), 8)
-            below = pl.ds(pl.multiple_of(rows + part * 8, 8), 8)
+    for part in range(rows // 8):
+        place, below = pl.ds(part * 8, 8), pl.ds(rows + part * 8, 8)
+        for rec in range(recs):
+            lanes = pl.ds(rec * LANES, LANES)
             out = real_forward([data_ref[shot, rec, place, :] for shot in range(shots)])
             for k in range(high + 1):
                 re, im = out[k]
                 held[k, place, lanes] = re
                 if k > 0:
                     held[k, below, lanes] = jnp.zeros_like(re) if im is None else im
-            return carry
-
-        lax.fori_loop(0, rows // 8, shots_forward, 0)
 
     def left_product(matrix, k):
         top, rest = split(held[k])
@@ -314,7 +312,7 @@
         for i in range(WAVES):
             for rec in range(recs):
                 n = (i * recs + rec) * rows
-                keep = distance >= (first + i) * bands_ref[first_rec + rec]
+                keep = distance >= (first + i) * bands[first_rec + rec]
                 kept.append(
                     jnp.concatenate(
                         [
@@ -336,23 +334,25 @@
             held[first + i] = left_product(outer_b, first + i)
         return carry
 
+    band_copy.wait()
     lax.fori_loop(0, high // WAVES, some_waves, 0)
 
-    for rec in range(recs):
-        lanes = pl.ds(rec * LANES, LANES)
-
-        def shots_backward(part, carry):
-            place = pl.ds(pl.multiple_of(part * 8, 8), 8)
-            below = pl.ds(pl.multiple_of(rows + part * 8, 8), 8)
+    copies = []
+    for part in range(rows // 8):
+        place, below = pl.ds(part * 8, 8), pl.ds(rows + part * 8, 8)
+        for rec in range(recs):
+            lanes = pl.ds(rec * LANES, LANES)
             spectrum = [(held[0, place, lanes] * (1.0 / shots), None)]
             for k in range(1, high + 1):
                 spectrum.append((held[k, place, lanes], held[k, below, lanes] if k < high else None))
             back = real_backward(spectrum, shots)
             for shot in range(shots):
                 out_ref[shot, pl.ds(part * (8 * recs) + rec, 8, stride=recs), :] = back[shot]
-            return carry
-
-        lax.fori_loop(0, rows // 8, shots_backward, 0)
+        done = pl.ds(part * (8 * recs), 8 * recs)
+        copies.append(pltpu.make_async_copy(out_ref.at[:, done], result_ref.at[:, done], sems.at[part]))
+        copies[-1].start()
+    for copy in copies:
+        copy.wait()
 
 
 def dip_filter(gathered, dip_band):
@@ -360,12 +360,18 @@
     out = pl.pallas_call(
         functools.partial(dip_kernel, (shots, recs, rows)),
         out_shape=jax.ShapeDtypeStruct((shots, rows * recs, LANES), jnp.float32),
-        in_specs=[whole(pltpu.SMEM)] + [whole()] * 6,
-        out_specs=whole(),
-        scratch_shapes=[pltpu.VMEM((shots // 2 + 1, 2 * rows, recs * LANES), jnp.float32)],
+        in_specs=[whole(pltpu.HBM)] + [whole()] * 6,
+        out_specs=whole(pltpu.HBM),
+        scratch_shapes=[
+            pltpu.VMEM((shots // 2 + 1, 2 * rows, recs * LANES), jnp.float32),
+            pltpu.VMEM((shots, rows * recs, LANES), jnp.float32),
+            pltpu.SMEM(dip_band.shape, jnp.int32),
+            pltpu.SemaphoreType.DMA,
+            pltpu.SemaphoreType.DMA((rows // 8,)),
+        ],
         compiler_params=pltpu.CompilerParams(vmem_limit_bytes=GRANT),
         name="dip",
-    )(dip_band, gathered, *tables(shots, rows))
+    )(pltpu.with_memory_space_constraint(dip_band, pltpu.HBM), gathered, *tables(shots, rows))
     return out.reshape(shots, rows, recs, LANES).transpose(0, 2, 1, 3).reshape(shots, recs, rows * LANES)
 
 

time: 60.8 us -> 56.5 us (0.929)
  local copies, waits for them, and re-layouts: 2.57 us -> 0.05 us
  Pallas kernels: 10.2 us -> 8.28 us
    unnamed x20 -> x16, local copies, waits for them, and re-layouts: 2.57 us -> 0.05 us
    pallas_call x1, Pallas kernels: 5.97 us -> 3.87 us  [dip_filter(): pl.pallas_call(functools.partial(dip_kernel, (shots, recs, rows)), out_sh...]
where the time goes in v2:
time: 56.5 us; the launch traced here: 56.3 us
  blocking collectives  20.2 us (36%)
  waiting for transfers between devices  14 us (25%)
  starting transfers between devices  13.6 us (24%)
  Pallas kernels  8.28 us (15%)
    all_to_all x1, blocking collectives, local(): lax.all_to_all(parted, 'shot', split_axis=0, concat_axis=0, tiled=True)  20.2 us
    ppermute x1, waiting for transfers between devices, local(): left = lax.ppermute(up, 'chan', [(i, i + 1) for i in range(blocks - 1)])  12.8 us
    ppermute x1, starting transfers between devices, local(): right = lax.ppermute(down, 'chan', [(i + 1, i) for i in range(blocks - 1)])  9.68 us
    ppermute x1, starting transfers between devices, local(): left = lax.ppermute(up, 'chan', [(i, i + 1) for i in range(blocks - 1)])  3.96 us
    pallas_call x1, Pallas kernels, dip_filter(): pl.pallas_call(functools.partial(dip_kernel, (shots, recs, rows)), out_sh...  3.87 us
    pallas_call x1, Pallas kernels, clean(): pl.pallas_call(functools.partial(clean_kernel, (shots, chans, rows)), out...  2.76 us
    pallas_call x1, Pallas kernels, align(): pl.pallas_call(functools.partial(align_kernel, (shots, chans, rows)), out...  1.66 us
    ppermute x1, waiting for transfers between devices, local(): right = lax.ppermute(down, 'chan', [(i + 1, i) for i in range(blocks - 1)])  1.18 us
  transfers between devices with their start and end apart: 2, of which 2 were waited for; matrix products, arithmetic and copies ran while one was open for 0% of the time, Pallas kernels for 0%

profile of v2, /device:TPU:24, one launch (start us, length us, event | category | flops | bytes accessed | tf_op | source)
XLA Modules:
  0.0 56.3 jit_solution(14871150673159210104)
XLA Ops:
  0.0 1.7 %align.1 = (f32[4,10,32,128]{3,2,1,0:T(8,128)S(1)}, f32[4,10,32,128]{3,2,1,0:T(8,128)S(1)}) custom-call(s32[4,16]{1,0:T(4,128)} %shifts_ref.3, f32[2048,128]{1,0:T(8,128)} %bitcast.12), custom_call_target="tpu_custom_call" | custom-call | tf_op jit(solution)/shard_map/align/pallas_call | solution.py:59
  1.7 0.0 copy-start.5
  1.7 0.0 copy-start.6
  1.7 0.0 copy-start.7
  1.7 4.0 %collective-permute-start = (f32[4,10,32,128]{3,2,1,0:T(8,128)S(1)}, f32[4,10,32,128]{3,2,1,0:T(8,128)S(1)}, u32[]{:S(2)}, u32[]{:S(2)}) collective-permute-start(f32[4,10,32,128]{3,2,1,0:T(8,128)S(1)} %get-tuple-element.7.up_ref), channel_id=1, source_target_pairs={{0,1},{1,2},{2,3},{3,4},{4,5},{5,6},{6,7},{7,8},{8,9},{9,10},{10,1... | collective-permute-start | bytes 1966088 | tf_op jit(solution)/shard_map/ppermute | solution.py:382
  5.7 9.7 %collective-permute-start.1 = (f32[4,10,32,128]{3,2,1,0:T(8,128)S(1)}, f32[4,10,32,128]{3,2,1,0:T(8,128)S(1)}, u32[]{:S(2)}, u32[]{:S(2)}) collective-permute-start(f32[4,10,32,128]{3,2,1,0:T(8,128)S(1)} %get-tuple-element.8.down_ref), channel_id=1, source_target_pairs={{1,0},{2,1},{3,2},{4,3},{5,4},{6,5},{7,6},{8,7},{9,8},{10,9},{11,1... | collective-permute-start | bytes 1966088 | tf_op jit(solution)/shard_map/ppermute | solution.py:383
  15.4 12.8 %collective-permute-done.left_ref = f32[4,10,32,128]{3,2,1,0:T(8,128)S(1)} collective-permute-done((f32[4,10,32,128]{3,2,1,0:T(8,128)S(1)}, f32[4,10,32,128]{3,2,1,0:T(8,128)S(1)}, u32[]{:S(2)}, u32[]{:S(2)}) %collective-permute-start) | collective-permute-done | bytes 655392 | tf_op jit(solution)/shard_map/ppermute | solution.py:382
  28.1 1.2 %collective-permute-done.1.right_ref = f32[4,10,32,128]{3,2,1,0:T(8,128)S(1)} collective-permute-done((f32[4,10,32,128]{3,2,1,0:T(8,128)S(1)}, f32[4,10,32,128]{3,2,1,0:T(8,128)S(1)}, u32[]{:S(2)}, u32[]{:S(2)}) %collective-permute-start.1) | collective-permute-done | bytes 655392 | tf_op jit(solution)/shard_map/ppermute | solution.py:383
  29.3 0.0 copy-done.5
  29.3 0.0 copy-done.6
  29.3 0.0 copy-done.7
  29.3 2.8 %clean.1 = f32[8,4,2,32,128]{4,3,2,1,0:T(8,128)S(1)} custom-call(s32[4,16]{1,0:T(4,128)S(1)} %copy-done.5, s32[16]{0:T(128)S(1)} %copy-done.6, s32[16]{0:T(128)S(1)} %copy-done.7, f32[4,10,32,128]{3,2,1,0:T(8,128)S(1)} %collective-permute-done.left_ref, f32[4,10,32,128]{3,2,1,0:T(8,128)S(1)} %get-tuple-element.8.down_ref, ...), custom_call_target="tpu_custom_call" | custom-call | tf_op jit(solution)/shard_map/clean/pallas_call | solution.py:169
  32.1 0.0 copy-start
  32.1 0.0 copy-start.1
  32.1 0.0 copy-start.2
  32.1 0.0 copy-start.3
  32.1 0.0 copy-start.4
  32.2 20.2 %all_to_all.5 = f32[8,4,2,32,128]{4,3,2,1,0:T(8,128)S(1)} all-to-all(f32[8,4,2,32,128]{4,3,2,1,0:T(8,128)S(1)} %clean.1), channel_id=1, replica_groups=mesh['shot'=8,'chan'=64] {'shot'}, dimensions={0} | all-to-all | bytes 2097152 | tf_op jit(solution)/shard_map/all_to_all | solution.py:385
  52.4 0.0 copy-done
  52.4 0.0 copy-done.1
  52.4 0.0 copy-done.2
  52.4 0.0 copy-done.3
  52.4 0.0 copy-done.4
  52.4 3.9 %dip.1 = f32[32,64,128]{2,1,0:T(8,128)} custom-call(s32[16]{0:T(128)} %bands_ref.1, f32[32,2,32,128]{3,2,1,0:T(8,128)S(1)} %bitcast.11, bf16[64,192]{1,0:T(8,128)(2,1)S(1)} %copy-done.4, bf16[64,192]{1,0:T(8,128)(2,1)S(1)} %copy-done.3, bf16[768,256]{1,0:T(8,128)(2,1)S(1)} %copy-done.1, bf16[768,256]{1,0:T(8,128)(2,1)S(1)} %copy-done, ...), custom_call_target="tpu_custom_call" | custom-call | tf_op jit(solution)/shard_map/dip/pallas_call | solution.py:360
Async XLA Ops:
  1.7 27.7 %copy-start.5 = (s32[4,16]{1,0:T(4,128)S(1)}, s32[4,16]{1,0:T(4,128)}, u32[]{:S(2)}) copy-start(s32[4,16]{1,0:T(4,128)} %shifts_ref.3) | copy-start | bytes 772
  1.7 27.6 %copy-start.6 = (s32[16]{0:T(128)S(1)}, s32[16]{0:T(128)}, u32[]{:S(2)}) copy-start(s32[16]{0:T(128)} %low_ref.1) | copy-start | bytes 196
  1.7 27.6 %copy-start.7 = (s32[16]{0:T(128)S(1)}, s32[16]{0:T(128)}, u32[]{:S(2)}) copy-start(s32[16]{0:T(128)} %high_ref.1) | copy-start | bytes 196
  1.7 26.4 %collective-permute-start = (f32[4,10,32,128]{3,2,1,0:T(8,128)S(1)}, f32[4,10,32,128]{3,2,1,0:T(8,128)S(1)}, u32[]{:S(2)}, u32[]{:S(2)}) collective-permute-start(f32[4,10,32,128]{3,2,1,0:T(8,128)S(1)} %get-tuple-element.7.up_ref), channel_id=1, source_target_pairs={{0,1},{1,2},{2,3},{3,4},{4,5},{5,6},{6,7},{7,8},{8,9},{9,10},{10,1... | collective-permute-start | bytes 1966088 | tf_op jit(solution)/shard_map/ppermute | solution.py:382
  5.7 23.7 %collective-permute-start.1 = (f32[4,10,32,128]{3,2,1,0:T(8,128)S(1)}, f32[4,10,32,128]{3,2,1,0:T(8,128)S(1)}, u32[]{:S(2)}, u32[]{:S(2)}) collective-permute-start(f32[4,10,32,128]{3,2,1,0:T(8,128)S(1)} %get-tuple-element.8.down_ref), channel_id=1, source_target_pairs={{1,0},{2,1},{3,2},{4,3},{5,4},{6,5},{7,6},{8,7},{9,8},{10,9},{11,1... | collective-permute-start | bytes 1966088 | tf_op jit(solution)/shard_map/ppermute | solution.py:383
  32.1 20.3 %copy-start = (bf16[768,256]{1,0:T(8,128)(2,1)S(1)}, bf16[768,256]{1,0:T(8,128)(2,1)}, u32[]{:S(2)}) copy-start(bf16[768,256]{1,0:T(8,128)(2,1)} %constant.13.clone.inner_b) | copy-start | bytes 1179652
  32.1 20.3 %copy-start.1 = (bf16[768,256]{1,0:T(8,128)(2,1)S(1)}, bf16[768,256]{1,0:T(8,128)(2,1)}, u32[]{:S(2)}) copy-start(bf16[768,256]{1,0:T(8,128)(2,1)} %constant.12.clone.inner_f) | copy-start | bytes 1179652
  32.1 20.3 %copy-start.2 = (f32[2,32,128]{2,1,0:T(8,128)S(1)}, f32[2,32,128]{2,1,0:T(8,128)}, u32[]{:S(2)}) copy-start(f32[2,32,128]{2,1,0:T(8,128)} %constant.14.clone.twist_ref) | copy-start | bytes 98308
  32.1 20.2 %copy-start.3 = (bf16[64,192]{1,0:T(8,128)(2,1)S(1)}, bf16[64,192]{1,0:T(8,128)(2,1)}, u32[]{:S(2)}) copy-start(bf16[64,192]{1,0:T(8,128)(2,1)} %constant.11.clone.outer_b) | copy-start | bytes 73732
  32.1 20.2 %copy-start.4 = (bf16[64,192]{1,0:T(8,128)(2,1)S(1)}, bf16[64,192]{1,0:T(8,128)(2,1)}, u32[]{:S(2)}) copy-start(bf16[64,192]{1,0:T(8,128)(2,1)} %constant.10.clone.outer_f) | copy-start | bytes 73732

commit v3 on v2

--- a/solution.py
+++ b/solution.py
@@ -8,6 +8,8 @@
 from jax.experimental.pallas import tpu as pltpu
 from jax.sharding import PartitionSpec as P
 
+
+PIECES = (1, 3)
 LANES = 128
 HALF = 5
 HALO = 2 * HALF
@@ -20,8 +22,10 @@
     return pl.BlockSpec(memory_space=space)
 
 
-def align_kernel(dims, shifts_ref, traces_ref, down_ref, up_ref, held, shifts, shift_sem, sems):
+def align_kernel(dims, pieces, shifts_ref, traces_ref, *refs):
+    edges, (held, shifts, shift_sem, sems) = refs[: 2 * len(pieces)], refs[2 * len(pieces) :]
     shots, chans, rows = dims
+    homes = [(piece, shot) for piece, count in enumerate(pieces) for shot in range(count)]
     tiles = chans * rows
     count = pltpu.make_async_copy(shifts_ref, shifts, shift_sem)
     count.start()
@@ -36,6 +40,8 @@
     count.wait()
     for shot in range(shots):
         copies[shot].wait()
+        piece, slot = homes[shot]
+        down_ref, up_ref = edges[2 * piece : 2 * piece + 2]
         for chan in range(chans):
             shift = shifts[shot, chan]
             part = shift & (LANES - 1)
@@ -46,21 +52,21 @@
             moved = pltpu.roll(mixed, (LANES - part) & (LANES - 1), 1)
             moved = jnp.where(sample < rows * LANES - shift, moved, 0.0)
             if chan < HALO:
-                down_ref[shot, chan] = moved
+                down_ref[slot, chan] = moved
             if chan >= chans - HALO:
-                up_ref[shot, chan - (chans - HALO)] = moved
-
-
-def align(traces, shifts):
+                up_ref[slot, chan - (chans - HALO)] = moved
+
+
+def align(traces, shifts, pieces):
     shots, chans, length = traces.shape
     rows = length // LANES
     flat = traces.reshape(shots, chans // 8, 8, rows, LANES).transpose(0, 1, 3, 2, 4).reshape(-1, LANES)
-    edge = jax.ShapeDtypeStruct((shots, HALO, rows, LANES), jnp.float32)
+    edges = [jax.ShapeDtypeStruct((count, HALO, rows, LANES), jnp.float32) for count in pieces for _ in range(2)]
     return pl.pallas_call(
-        functools.partial(align_kernel, (shots, chans, rows)),
-        out_shape=(edge, edge),
+        functools.partial(align_kernel, (shots, chans, rows), pieces),
+        out_shape=tuple(edges),
         in_specs=[whole(pltpu.HBM), whole(pltpu.HBM)],
-        out_specs=(whole(), whole()),
+        out_specs=(whole(),) * len(edges),
         scratch_shapes=[
             pltpu.VMEM((shots, chans * rows + TAIL, LANES), jnp.float32),
             pltpu.SMEM((shots, chans), jnp.int32),
@@ -126,9 +132,9 @@
     return result
 
 
-def clean_kernel(dims, shifts_ref, low_ref, high_ref, left_ref, down_ref, up_ref, right_ref, out_ref, held):
+def clean_kernel(dims, start, shots_here, shifts_ref, low_ref, high_ref, left_ref, down_ref, up_ref, right_ref, out_ref, held):
     shots, chans, rows = dims
-    first_shot = lax.axis_index("shot") * shots
+    first_shot = lax.axis_index("shot") * shots_here + start
     lead = 8
     for chan in range(chans):
         held[chan, pl.ds(0, lead), :] = jnp.zeros((lead, LANES), jnp.float32)
@@ -151,7 +157,7 @@
 
         lax.fori_loop(0, rows // 8, one_part, 0)
         for chan in range(chans):
-            shift = shifts_ref[shot, chan]
+            shift = shifts_ref[start + shot, chan]
             whole_rows, part = shift >> 7, shift & (LANES - 1)
             inside = (first_shot + shot >= low_ref[chan]) & (first_shot + shot < high_ref[chan])
             first = held[chan, pl.ds(lead - whole_rows, rows), :]
@@ -164,10 +170,11 @@
     lax.fori_loop(0, shots, one_shot, 0)
 
 
-def clean(shifts, low, high, left, down, up, right, chans, groups):
+def clean(shifts, low, high, left, down, up, right, start, groups):
     shots, _, rows, _ = down.shape
+    shots_here, chans = shifts.shape
     return pl.pallas_call(
-        functools.partial(clean_kernel, (shots, chans, rows)),
+        functools.partial(clean_kernel, (shots, chans, rows), start, shots_here),
         out_shape=jax.ShapeDtypeStruct((groups, shots, chans // groups, rows, LANES), jnp.float32),
         in_specs=[whole(pltpu.SMEM)] * 3 + [whole()] * 4,
         out_specs=whole(),
@@ -268,7 +275,9 @@
     return jnp.dot(a, b, preferred_element_type=jnp.float32)
 
 
-def dip_kernel(dims, bands_ref, data_ref, outer_f, outer_b, inner_f, inner_b, twist_ref, result_ref, held, out_ref, bands, band_sem, sems):
+def dip_kernel(dims, pieces, bands_ref, *refs):
+    data_refs, refs = refs[: len(pieces)], refs[len(pieces) :]
+    outer_f, outer_b, inner_f, inner_b, twist_ref, result_ref, held, out_ref, bands, band_sem, sems = refs
     shots, recs, rows = dims
     high = shots // 2
     band_copy = pltpu.make_async_copy(bands_ref, bands, band_sem)
@@ -282,7 +291,13 @@
         place, below = pl.ds(part * 8, 8), pl.ds(rows + part * 8, 8)
         for rec in range(recs):
             lanes = pl.ds(rec * LANES, LANES)
-            out = real_forward([data_ref[shot, rec, place, :] for shot in range(shots)])
+            gathered = [
+                data_refs[piece][group, slot, rec, place, :]
+                for group in range(shots // sum(pieces))
+                for piece, count in enumerate(pieces)
+                for slot in range(count)
+            ]
+            out = real_forward(gathered)
             for k in range(high + 1):
                 re, im = out[k]
                 held[k, place, lanes] = re
@@ -356,11 +371,13 @@
 
 
 def dip_filter(gathered, dip_band):
-    shots, recs, rows, _ = gathered.shape
+    groups, _, recs, rows, _ = gathered[0].shape
+    pieces = tuple(piece.shape[1] for piece in gathered)
+    shots = groups * sum(pieces)
     out = pl.pallas_call(
-        functools.partial(dip_kernel, (shots, recs, rows)),
+        functools.partial(dip_kernel, (shots, recs, rows), pieces),
         out_shape=jax.ShapeDtypeStruct((shots, rows * recs, LANES), jnp.float32),
-        in_specs=[whole(pltpu.HBM)] + [whole()] * 6,
+        in_specs=[whole(pltpu.HBM)] + [whole()] * (5 + len(gathered)),
         out_specs=whole(pltpu.HBM),
         scratch_shapes=[
             pltpu.VMEM((shots // 2 + 1, 2 * rows, recs * LANES), jnp.float32),
@@ -371,20 +388,25 @@
         ],
         compiler_params=pltpu.CompilerParams(vmem_limit_bytes=GRANT),
         name="dip",
-    )(pltpu.with_memory_space_constraint(dip_band, pltpu.HBM), gathered, *tables(shots, rows))
+    )(pltpu.with_memory_space_constraint(dip_band, pltpu.HBM), *gathered, *tables(shots, rows))
     return out.reshape(shots, rows, recs, LANES).transpose(0, 2, 1, 3).reshape(shots, recs, rows * LANES)
 
 
 def local(traces, shifts, aperture_lo, aperture_hi, dip_band):
-    shots, chans, length = traces.shape
     blocks, groups = lax.axis_size("chan"), lax.axis_size("shot")
-    down, up = align(traces, shifts)
-    left = lax.ppermute(up, "chan", [(i, i + 1) for i in range(blocks - 1)])
-    right = lax.ppermute(down, "chan", [(i + 1, i) for i in range(blocks - 1)])
-    parted = clean(shifts, aperture_lo, aperture_hi, left, down, up, right, chans, groups)
-    arrived = lax.all_to_all(parted, "shot", split_axis=0, concat_axis=0, tiled=True)
-    gathered = arrived.reshape(groups * shots, chans // groups, length // LANES, LANES)
-    return dip_filter(gathered, dip_band)
+    upward, downward = [(i, i + 1) for i in range(blocks - 1)], [(i + 1, i) for i in range(blocks - 1)]
+    edges = align(traces, shifts, PIECES)
+    sides = []
+    for i in range(len(PIECES)):
+        down, up = edges[2 * i : 2 * i + 2]
+        left = lax.ppermute(up, "chan", upward)
+        right = lax.ppermute(down, "chan", downward)
+        sides.append((left, down, up, right))
+    arrived = []
+    for i in range(len(PIECES)):
+        parted = clean(shifts, aperture_lo, aperture_hi, *sides[i], sum(PIECES[:i]), groups)
+        arrived.append(lax.all_to_all(parted, "shot", split_axis=0, concat_axis=0, tiled=True))
+    return dip_filter(arrived, dip_band)
 
 
 def solution(mesh):

time: 56.5 us -> 62.6 us (1.11)
  starting transfers between devices: 13.6 us -> 25.8 us
  blocking collectives: 20.2 us -> 15.6 us
  waiting for transfers between devices: 14 us -> 11.2 us
  Pallas kernels: 8.28 us -> 9.57 us
    ppermute x2 -> x4, waiting for transfers between devices: 14 us -> 5.98 us  [the longest x2 4.79 us: local(): left = lax.ppermute(up, 'chan', upward)]
    ppermute x2 -> x4, starting transfers between devices: 13.6 us -> 21.5 us  [the longest x2 15.7 us: local(): right = lax.ppermute(down, 'chan', downward)]
    all_to_all x0 -> x1, waiting for transfers between devices: none -> 5.21 us  [local(): lax.all_to_all(parted, 'shot', split_axis=0, concat_axis=0, tiled=True)]
    all_to_all x1, blocking collectives: 20.2 us -> 15.6 us  [local(): lax.all_to_all(parted, 'shot', split_axis=0, concat_axis=0, tiled=True)]
    all_to_all x0 -> x1, starting transfers between devices: none -> 4.3 us  [local(): lax.all_to_all(parted, 'shot', split_axis=0, concat_axis=0, tiled=True)]
    pallas_call x3 -> x4, Pallas kernels: 8.28 us -> 9.57 us  [the longest x2 4.05 us: clean(): pl.pallas_call(functools.partial(clean_kernel, (shots, chans, rows), star...]
  transfers between devices with their start and end apart: 2 -> 5, of which waited for: 2 -> 3; matrix products, arithmetic and copies ran while one was open for 0% -> 0% of each run, Pallas kernels for 0% -> 6%
where the time goes in v3:
time: 62.6 us; the launch traced here: 62.3 us
  starting transfers between devices  25.8 us (41%)
  blocking collectives  15.6 us (25%)
  waiting for transfers between devices  11.2 us (18%)
  Pallas kernels  9.57 us (15%)
    ppermute x2, starting transfers between devices, local(): right = lax.ppermute(down, 'chan', downward)  15.7 us
    all_to_all x1, blocking collectives, local(): lax.all_to_all(parted, 'shot', split_axis=0, concat_axis=0, tiled=True)  15.6 us
    ppermute x2, starting transfers between devices, local(): left = lax.ppermute(up, 'chan', upward)  5.75 us
    all_to_all x1, waiting for transfers between devices, local(): lax.all_to_all(parted, 'shot', split_axis=0, concat_axis=0, tiled=True)  5.21 us
    ppermute x2, waiting for transfers between devices, local(): left = lax.ppermute(up, 'chan', upward)  4.79 us
    all_to_all x1, starting transfers between devices, local(): lax.all_to_all(parted, 'shot', split_axis=0, concat_axis=0, tiled=True)  4.3 us
    pallas_call x2, Pallas kernels, clean(): pl.pallas_call(functools.partial(clean_kernel, (shots, chans, rows), star...  4.05 us
    pallas_call x1, Pallas kernels, dip_filter(): pl.pallas_call(functools.partial(dip_kernel, (shots, recs, rows), pieces)...  3.87 us
  transfers between devices with their start and end apart: 5, of which 3 were waited for; matrix products, arithmetic and copies ran while one was open for 0% of the time, Pallas kernels for 6%

profile of v3, /device:TPU:24, one launch (start us, length us, event | category | flops | bytes accessed | tf_op | source)
XLA Modules:
  0.0 62.3 jit_solution(12236971771586316464)
XLA Ops:
  0.0 1.7 %align.1 = (f32[1,10,32,128]{3,2,1,0:T(8,128)S(1)}, f32[1,10,32,128]{3,2,1,0:T(8,128)S(1)}, f32[3,10,32,128]{3,2,1,0:T(8,128)S(1)}, f32[3,10,32,128]{3,2,1,0:T(8,128)S(1)}) custom-call(s32[4,16]{1,0:T(4,128)} %shifts_ref.5, f32[2048,128]{1,0:T(8,128)} %bitcast.10), custom_call_target="tpu_custom_call" | custom-call | tf_op jit(solution)/shard_map/align/pallas_call | solution.py:65
  1.7 3.8 %collective-permute-start.2 = (f32[3,10,32,128]{3,2,1,0:T(8,128)S(1)}, f32[3,10,32,128]{3,2,1,0:T(8,128)S(1)}, u32[]{:S(2)}, u32[]{:S(2)}) collective-permute-start(f32[3,10,32,128]{3,2,1,0:T(8,128)S(1)} %get-tuple-element.11.up_ref), channel_id=1, source_target_pairs={{0,1},{1,2},{2,3},{3,4},{4,5},{5,6},{6,7},{7,8},{8,9},{9,10},{10,1... | collective-permute-start | bytes 1474568 | tf_op jit(solution)/shard_map/ppermute | solution.py:402
  5.5 0.0 copy-start.5
  5.5 9.7 %collective-permute-start.3 = (f32[3,10,32,128]{3,2,1,0:T(8,128)S(1)}, f32[3,10,32,128]{3,2,1,0:T(8,128)S(1)}, u32[]{:S(2)}, u32[]{:S(2)}) collective-permute-start(f32[3,10,32,128]{3,2,1,0:T(8,128)S(1)} %get-tuple-element.12.down_ref), channel_id=1, source_target_pairs={{1,0},{2,1},{3,2},{4,3},{5,4},{6,5},{7,6},{8,7},{9,8},{10,9},{11,1... | collective-permute-start | bytes 1474568 | tf_op jit(solution)/shard_map/ppermute | solution.py:403
  15.2 0.0 copy-start.6
  15.2 0.0 copy-start.7
  15.2 1.9 %collective-permute-start = (f32[1,10,32,128]{3,2,1,0:T(8,128)S(1)}, f32[1,10,32,128]{3,2,1,0:T(8,128)S(1)}, u32[]{:S(2)}, u32[]{:S(2)}) collective-permute-start(f32[1,10,32,128]{3,2,1,0:T(8,128)S(1)} %get-tuple-element.9.up_ref), channel_id=1, source_target_pairs={{0,1},{1,2},{2,3},{3,4},{4,5},{5,6},{6,7},{7,8},{8,9},{9,10},{10,1... | collective-permute-start | bytes 491528 | tf_op jit(solution)/shard_map/ppermute | solution.py:402
  17.1 6.0 %collective-permute-start.1 = (f32[1,10,32,128]{3,2,1,0:T(8,128)S(1)}, f32[1,10,32,128]{3,2,1,0:T(8,128)S(1)}, u32[]{:S(2)}, u32[]{:S(2)}) collective-permute-start(f32[1,10,32,128]{3,2,1,0:T(8,128)S(1)} %get-tuple-element.10.down_ref), channel_id=1, source_target_pairs={{1,0},{2,1},{3,2},{4,3},{5,4},{6,5},{7,6},{8,7},{9,8},{10,9},{11,1... | collective-permute-start | bytes 491528 | tf_op jit(solution)/shard_map/ppermute | solution.py:403
  23.2 4.8 %collective-permute-done.left_ref = f32[1,10,32,128]{3,2,1,0:T(8,128)S(1)} collective-permute-done((f32[1,10,32,128]{3,2,1,0:T(8,128)S(1)}, f32[1,10,32,128]{3,2,1,0:T(8,128)S(1)}, u32[]{:S(2)}, u32[]{:S(2)}) %collective-permute-start) | collective-permute-done | bytes 163872 | tf_op jit(solution)/shard_map/ppermute | solution.py:402
  28.0 1.2 %collective-permute-done.1.right_ref = f32[1,10,32,128]{3,2,1,0:T(8,128)S(1)} collective-permute-done((f32[1,10,32,128]{3,2,1,0:T(8,128)S(1)}, f32[1,10,32,128]{3,2,1,0:T(8,128)S(1)}, u32[]{:S(2)}, u32[]{:S(2)}) %collective-permute-start.1) | collective-permute-done | bytes 163872 | tf_op jit(solution)/shard_map/ppermute | solution.py:403
  29.2 0.0 copy-done.7
  29.2 1.8 %clean.2 = f32[8,1,2,32,128]{4,3,2,1,0:T(8,128)} custom-call(s32[4,16]{1,0:T(4,128)S(1)} %copy-done.5, s32[16]{0:T(128)S(1)} %copy-done.6, s32[16]{0:T(128)S(1)} %copy-done.7, f32[1,10,32,128]{3,2,1,0:T(8,128)S(1)} %collective-permute-done.left_ref, f32[1,10,32,128]{3,2,1,0:T(8,128)S(1)} %get-tuple-element.10.down_ref, ...), custom_call_target="tpu_custom_call" | custom-call | tf_op jit(solution)/shard_map/clean/pallas_call | solution.py:176
  31.0 4.3 %all-to-all-start = ((f32[8,1,2,32,128]{4,3,2,1,0:T(8,128)}), f32[8,1,2,32,128]{4,3,2,1,0:T(8,128)S(1)}, u32[]{:S(2)}, u32[]{:S(2)}) async-start(f32[8,1,2,32,128]{4,3,2,1,0:T(8,128)} %clean.2), calls=%async_computation | async-start | bytes 524288 | tf_op jit(solution)/shard_map/all_to_all | solution.py:408
  35.3 0.0 collective-permute-done.2.left_ref
  35.3 0.0 collective-permute-done.3.right_ref
  35.3 2.2 %clean.3 = f32[8,3,2,32,128]{4,3,2,1,0:T(8,128)S(1)} custom-call(s32[4,16]{1,0:T(4,128)S(1)} %copy-done.5, s32[16]{0:T(128)S(1)} %copy-done.6, s32[16]{0:T(128)S(1)} %copy-done.7, f32[3,10,32,128]{3,2,1,0:T(8,128)S(1)} %collective-permute-done.2.left_ref, f32[3,10,32,128]{3,2,1,0:T(8,128)S(1)} %get-tuple-element.12.down_ref, ...), custom_call_target="tpu_custom_call" | custom-call | tf_op jit(solution)/shard_map/clean/pallas_call | solution.py:176
  37.5 0.0 copy-start
  37.6 0.0 copy-start.1
  37.6 0.0 copy-start.2
  37.6 0.0 copy-start.3
  37.6 0.0 copy-start.4
  37.6 5.2 %all-to-all-done.refs_0_ = f32[8,1,2,32,128]{4,3,2,1,0:T(8,128)S(1)} async-done(((f32[8,1,2,32,128]{4,3,2,1,0:T(8,128)}), f32[8,1,2,32,128]{4,3,2,1,0:T(8,128)S(1)}, u32[]{:S(2)}, u32[]{:S(2)}) %all-to-all-start) | async-done | bytes 262176 | tf_op jit(solution)/shard_map/all_to_all | solution.py:408
  42.8 15.6 %all_to_all.10.refs_1_ = f32[8,3,2,32,128]{4,3,2,1,0:T(8,128)S(1)} all-to-all(f32[8,3,2,32,128]{4,3,2,1,0:T(8,128)S(1)} %clean.3), channel_id=1, replica_groups=mesh['shot'=8,'chan'=64] {'shot'}, dimensions={0} | all-to-all | bytes 1572864 | tf_op jit(solution)/shard_map/all_to_all | solution.py:408
  58.4 3.9 %dip.1 = f32[32,64,128]{2,1,0:T(8,128)} custom-call(s32[16]{0:T(128)} %bands_ref.1, f32[8,1,2,32,128]{4,3,2,1,0:T(8,128)S(1)} %all-to-all-done.refs_0_, f32[8,3,2,32,128]{4,3,2,1,0:T(8,128)S(1)} %all_to_all.10.refs_1_, bf16[64,192]{1,0:T(8,128)(2,1)S(1)} %copy-done.4, bf16[64,192]{1,0:T(8,128)(2,1)S(1)} %copy-done.3, bf16[768,256]{1,0:T(8,128)(2,1)S(1)} %copy-done.1, ...), custom_call_target="tpu_custom_call" | custom-call | tf_op jit(solution)/shard_map/dip/pallas_call | solution.py:377
  (7 shorter events, 0.0 us)
Async XLA Ops:
  1.7 33.6 %collective-permute-start.2 = (f32[3,10,32,128]{3,2,1,0:T(8,128)S(1)}, f32[3,10,32,128]{3,2,1,0:T(8,128)S(1)}, u32[]{:S(2)}, u32[]{:S(2)}) collective-permute-start(f32[3,10,32,128]{3,2,1,0:T(8,128)S(1)} %get-tuple-element.11.up_ref), channel_id=1, source_target_pairs={{0,1},{1,2},{2,3},{3,4},{4,5},{5,6},{6,7},{7,8},{8,9},{9,10},{10,1... | collective-permute-start | bytes 1474568 | tf_op jit(solution)/shard_map/ppermute | solution.py:402
  5.5 23.7 %copy-start.5 = (s32[4,16]{1,0:T(4,128)S(1)}, s32[4,16]{1,0:T(4,128)}, u32[]{:S(2)}) copy-start(s32[4,16]{1,0:T(4,128)} %shifts_ref.5) | copy-start | bytes 772
  5.5 29.8 %collective-permute-start.3 = (f32[3,10,32,128]{3,2,1,0:T(8,128)S(1)}, f32[3,10,32,128]{3,2,1,0:T(8,128)S(1)}, u32[]{:S(2)}, u32[]{:S(2)}) collective-permute-start(f32[3,10,32,128]{3,2,1,0:T(8,128)S(1)} %get-tuple-element.12.down_ref), channel_id=1, source_target_pairs={{1,0},{2,1},{3,2},{4,3},{5,4},{6,5},{7,6},{8,7},{9,8},{10,9},{11,1... | collective-permute-start | bytes 1474568 | tf_op jit(solution)/shard_map/ppermute | solution.py:403
  15.2 14.0 %copy-start.6 = (s32[16]{0:T(128)S(1)}, s32[16]{0:T(128)}, u32[]{:S(2)}) copy-start(s32[16]{0:T(128)} %low_ref.3) | copy-start | bytes 196
  15.2 14.0 %copy-start.7 = (s32[16]{0:T(128)S(1)}, s32[16]{0:T(128)}, u32[]{:S(2)}) copy-start(s32[16]{0:T(128)} %high_ref.3) | copy-start | bytes 196
  15.2 12.8 %collective-permute-start = (f32[1,10,32,128]{3,2,1,0:T(8,128)S(1)}, f32[1,10,32,128]{3,2,1,0:T(8,128)S(1)}, u32[]{:S(2)}, u32[]{:S(2)}) collective-permute-start(f32[1,10,32,128]{3,2,1,0:T(8,128)S(1)} %get-tuple-element.9.up_ref), channel_id=1, source_target_pairs={{0,1},{1,2},{2,3},{3,4},{4,5},{5,6},{6,7},{7,8},{8,9},{9,10},{10,1... | collective-permute-start | bytes 491528 | tf_op jit(solution)/shard_map/ppermute | solution.py:402
  17.1 12.0 %collective-permute-start.1 = (f32[1,10,32,128]{3,2,1,0:T(8,128)S(1)}, f32[1,10,32,128]{3,2,1,0:T(8,128)S(1)}, u32[]{:S(2)}, u32[]{:S(2)}) collective-permute-start(f32[1,10,32,128]{3,2,1,0:T(8,128)S(1)} %get-tuple-element.10.down_ref), channel_id=1, source_target_pairs={{1,0},{2,1},{3,2},{4,3},{5,4},{6,5},{7,6},{8,7},{9,8},{10,9},{11,1... | collective-permute-start | bytes 491528 | tf_op jit(solution)/shard_map/ppermute | solution.py:403
  31.0 11.8 %all-to-all-start = ((f32[8,1,2,32,128]{4,3,2,1,0:T(8,128)}), f32[8,1,2,32,128]{4,3,2,1,0:T(8,128)S(1)}, u32[]{:S(2)}, u32[]{:S(2)}) async-start(f32[8,1,2,32,128]{4,3,2,1,0:T(8,128)} %clean.2), calls=%async_computation | async-start | bytes 524288 | tf_op jit(solution)/shard_map/all_to_all | solution.py:408
  37.5 20.8 %copy-start = (bf16[768,256]{1,0:T(8,128)(2,1)S(1)}, bf16[768,256]{1,0:T(8,128)(2,1)}, u32[]{:S(2)}) copy-start(bf16[768,256]{1,0:T(8,128)(2,1)} %constant.13.clone.refs_5_) | copy-start | bytes 1179652
  37.6 20.8 %copy-start.1 = (bf16[768,256]{1,0:T(8,128)(2,1)S(1)}, bf16[768,256]{1,0:T(8,128)(2,1)}, u32[]{:S(2)}) copy-start(bf16[768,256]{1,0:T(8,128)(2,1)} %constant.12.clone.refs_4_) | copy-start | bytes 1179652
  37.6 20.8 %copy-start.2 = (f32[2,32,128]{2,1,0:T(8,128)S(1)}, f32[2,32,128]{2,1,0:T(8,128)}, u32[]{:S(2)}) copy-start(f32[2,32,128]{2,1,0:T(8,128)} %constant.14.clone.refs_6_) | copy-start | bytes 98308
  37.6 20.8 %copy-start.3 = (bf16[64,192]{1,0:T(8,128)(2,1)S(1)}, bf16[64,192]{1,0:T(8,128)(2,1)}, u32[]{:S(2)}) copy-start(bf16[64,192]{1,0:T(8,128)(2,1)} %constant.11.clone.refs_3_) | copy-start | bytes 73732
  37.6 20.8 %copy-start.4 = (bf16[64,192]{1,0:T(8,128)(2,1)S(1)}, bf16[64,192]{1,0:T(8,128)(2,1)}, u32[]{:S(2)}) copy-start(bf16[64,192]{1,0:T(8,128)(2,1)} %constant.10.clone.refs_2_) | copy-start | bytes 73732

commit v4 on v3

--- a/solution.py
+++ b/solution.py
@@ -15,6 +15,7 @@
 HALO = 2 * HALF
 TAIL = 8 * 9
 GRANT = 16 << 20
+PARTS = 2
 WAVES = 16
 
 
@@ -39,7 +40,9 @@
     sample = lax.broadcasted_iota(jnp.int32, (rows, LANES), 0) * LANES + lane
     count.wait()
     for shot in range(shots):
-        copies[shot].wait()
+        if shot < 2:
+            for copy in copies[shot : 1 + shot * shots]:
+                copy.wait()
         piece, slot = homes[shot]
         down_ref, up_ref = edges[2 * piece : 2 * piece + 2]
         for chan in range(chans):
@@ -136,38 +139,41 @@
     shots, chans, rows = dims
     first_shot = lax.axis_index("shot") * shots_here + start
     lead = 8
-    for chan in range(chans):
-        held[chan, pl.ds(0, lead), :] = jnp.zeros((lead, LANES), jnp.float32)
+    for slot in range(2):
+        for chan in range(chans):
+            held[slot, chan, pl.ds(0, lead), :] = jnp.zeros((lead, LANES), jnp.float32)
     lane = lax.broadcasted_iota(jnp.int32, (rows, LANES), 1)
 
-    def one_shot(shot, carry):
-        def one_part(part, inner):
-            place = pl.ds(pl.multiple_of(part * 8, 8), 8)
-            values = [left_ref[shot, i, place, :] for i in range(HALO)]
-            values += [down_ref[shot, i, place, :] for i in range(HALO)]
-            values += [up_ref[shot, i, place, :] for i in range(2 * HALO - chans, HALO)]
-            values += [right_ref[shot, i, place, :] for i in range(HALO)]
-            once = medians(values, chans + HALO)
-            once = [values[HALF + i] - once[i] for i in range(chans + HALO)]
-            twice = medians(once, chans)
-            stored = pl.ds(pl.multiple_of(lead + part * 8, 8), 8)
-            for i in range(chans):
-                held[i, stored, :] = once[HALF + i] - twice[i]
-            return inner
-
-        lax.fori_loop(0, rows // 8, one_part, 0)
-        for chan in range(chans):
-            shift = shifts_ref[start + shot, chan]
-            whole_rows, part = shift >> 7, shift & (LANES - 1)
-            inside = (first_shot + shot >= low_ref[chan]) & (first_shot + shot < high_ref[chan])
-            first = held[chan, pl.ds(lead - whole_rows, rows), :]
-            second = held[chan, pl.ds(lead - 1 - whole_rows, rows), :]
-            mixed = jnp.where(lane < LANES - part, first, second)
-            moved = pltpu.roll(mixed, part, 1)
-            out_ref[chan // 2, shot, chan % 2] = jnp.where(inside, moved, 0.0)
-        return carry
-
-    lax.fori_loop(0, shots, one_shot, 0)
+    def passes(shot, part):
+        place = pl.ds(part * 8, 8)
+        values = [left_ref[shot, i, place, :] for i in range(HALO)]
+        values += [down_ref[shot, i, place, :] for i in range(HALO)]
+        values += [up_ref[shot, i, place, :] for i in range(2 * HALO - chans, HALO)]
+        values += [right_ref[shot, i, place, :] for i in range(HALO)]
+        once = medians(values, chans + HALO)
+        once = [values[HALF + i] - once[i] for i in range(chans + HALO)]
+        twice = medians(once, chans)
+        for i in range(chans):
+            held[shot % 2, i, pl.ds(lead + part * 8, 8), :] = once[HALF + i] - twice[i]
+
+    def restore(shot, chan):
+        shift = shifts_ref[start + shot, chan]
+        whole_rows, part = shift >> 7, shift & (LANES - 1)
+        inside = (first_shot + shot >= low_ref[chan]) & (first_shot + shot < high_ref[chan])
+        first = held[shot % 2, chan, pl.ds(lead - whole_rows, rows), :]
+        second = held[shot % 2, chan, pl.ds(lead - 1 - whole_rows, rows), :]
+        mixed = jnp.where(lane < LANES - part, first, second)
+        moved = pltpu.roll(mixed, part, 1)
+        out_ref[chan // 2, shot, chan % 2] = jnp.where(inside, moved, 0.0)
+
+    parts = rows // 8
+    for shot in range(shots + 1):
+        for part in range(parts):
+            if shot < shots:
+                passes(shot, part)
+            if shot > 0:
+                for chan in range(part * chans // parts, (part + 1) * chans // parts):
+                    restore(shot - 1, chan)
 
 
 def clean(shifts, low, high, left, down, up, right, start, groups):
@@ -178,7 +184,7 @@
         out_shape=jax.ShapeDtypeStruct((groups, shots, chans // groups, rows, LANES), jnp.float32),
         in_specs=[whole(pltpu.SMEM)] * 3 + [whole()] * 4,
         out_specs=whole(),
-        scratch_shapes=[pltpu.VMEM((chans, 8 + rows, LANES), jnp.float32)],
+        scratch_shapes=[pltpu.VMEM((2, chans, 8 + rows, LANES), jnp.float32)],
         compiler_params=pltpu.CompilerParams(vmem_limit_bytes=GRANT),
         name="clean",
     )(shifts, low, high, left, down, up, right)
@@ -309,10 +315,14 @@
         return dot(matrix[...], jnp.concatenate([top, rest, top], axis=0))
 
     def right_product(lines, matrix):
-        top, rest = split(lines)
-        return dot(jnp.concatenate([top, rest, top], axis=1), matrix[...])
-
-    def some_waves(step, carry):
+        size = len(lines) // PARTS
+        done = []
+        for i in range(PARTS):
+            top, rest = split(jnp.concatenate(lines[i * size : (i + 1) * size], axis=0))
+            done.append(dot(jnp.concatenate([top, rest, top], axis=1), matrix[...]))
+        return jnp.concatenate(done, axis=0)
+
+    def some_waves(step):
         cos, sin = twist_ref[0], twist_ref[1]
         first = 1 + step * WAVES
         lines = []
@@ -322,7 +332,7 @@
                 mine = slice(rec * LANES, (rec + 1) * LANES)
                 re, im = spec[:rows, mine], spec[rows:, mine]
                 lines.append(jnp.concatenate([re * cos + im * sin, im * cos - re * sin], axis=1))
-        wave = right_product(jnp.concatenate(lines, axis=0), inner_f)
+        wave = right_product(lines, inner_f)
         kept = []
         for i in range(WAVES):
             for rec in range(recs):
@@ -337,7 +347,7 @@
                         axis=1,
                     )
                 )
-        wave = right_product(jnp.concatenate(kept, axis=0), inner_b)
+        wave = right_product(kept, inner_b)
         for i in range(WAVES):
             for rec in range(recs):
                 n = (i * recs + rec) * rows
@@ -347,10 +357,10 @@
                 held[first + i, rows:, lanes] = im * cos + re * sin
         for i in range(WAVES):
             held[first + i] = left_product(outer_b, first + i)
-        return carry
 
     band_copy.wait()
-    lax.fori_loop(0, high // WAVES, some_waves, 0)
+    for step in range(high // WAVES):
+        some_waves(step)
 
     copies = []
     for part in range(rows // 8):

time: 62.6 us -> 62.1 us (level)
  Pallas kernels: 9.57 us -> 8.61 us
where the time goes in v4:
time: 62.1 us; the launch traced here: 61.7 us
  starting transfers between devices  25.8 us (42%)
  blocking collectives  15.6 us (25%)
  waiting for transfers between devices  11.6 us (19%)
  Pallas kernels  8.61 us (14%)
    ppermute x2, starting transfers between devices, local(): right = lax.ppermute(down, 'chan', downward)  15.7 us
    all_to_all x1, blocking collectives, local(): lax.all_to_all(parted, 'shot', split_axis=0, concat_axis=0, tiled=True)  15.6 us
    ppermute x2, starting transfers between devices, local(): left = lax.ppermute(up, 'chan', upward)  5.75 us
    all_to_all x1, waiting for transfers between devices, local(): lax.all_to_all(parted, 'shot', split_axis=0, concat_axis=0, tiled=True)  5.59 us
    ppermute x2, waiting for transfers between devices, local(): left = lax.ppermute(up, 'chan', upward)  4.79 us
    all_to_all x1, starting transfers between devices, local(): lax.all_to_all(parted, 'shot', split_axis=0, concat_axis=0, tiled=True)  4.3 us
    pallas_call x2, Pallas kernels, clean(): pl.pallas_call(functools.partial(clean_kernel, (shots, chans, rows), star...  3.61 us
    pallas_call x1, Pallas kernels, dip_filter(): pl.pallas_call(functools.partial(dip_kernel, (shots, recs, rows), pieces)...  3.41 us
  transfers between devices with their start and end apart: 5, of which 3 were waited for; matrix products, arithmetic and copies ran while one was open for 0% of the time, Pallas kernels for 6%

profile of v4, /device:TPU:24, one launch (start us, length us, event | category | flops | bytes accessed | tf_op | source)
XLA Modules:
  0.0 61.7 jit_solution(13578915126594806567)
XLA Ops:
  0.0 1.6 %align.1 = (f32[1,10,32,128]{3,2,1,0:T(8,128)S(1)}, f32[1,10,32,128]{3,2,1,0:T(8,128)S(1)}, f32[3,10,32,128]{3,2,1,0:T(8,128)S(1)}, f32[3,10,32,128]{3,2,1,0:T(8,128)S(1)}) custom-call(s32[4,16]{1,0:T(4,128)} %shifts_ref.5, f32[2048,128]{1,0:T(8,128)} %bitcast.10), custom_call_target="tpu_custom_call" | custom-call | tf_op jit(solution)/shard_map/align/pallas_call | solution.py:68
  1.6 3.8 %collective-permute-start.2 = (f32[3,10,32,128]{3,2,1,0:T(8,128)S(1)}, f32[3,10,32,128]{3,2,1,0:T(8,128)S(1)}, u32[]{:S(2)}, u32[]{:S(2)}) collective-permute-start(f32[3,10,32,128]{3,2,1,0:T(8,128)S(1)} %get-tuple-element.11.up_ref), channel_id=1, source_target_pairs={{0,1},{1,2},{2,3},{3,4},{4,5},{5,6},{6,7},{7,8},{8,9},{9,10},{10,1... | collective-permute-start | bytes 1474568 | tf_op jit(solution)/shard_map/ppermute | solution.py:412
  5.4 0.0 copy-start.5
  5.4 9.7 %collective-permute-start.3 = (f32[3,10,32,128]{3,2,1,0:T(8,128)S(1)}, f32[3,10,32,128]{3,2,1,0:T(8,128)S(1)}, u32[]{:S(2)}, u32[]{:S(2)}) collective-permute-start(f32[3,10,32,128]{3,2,1,0:T(8,128)S(1)} %get-tuple-element.12.down_ref), channel_id=1, source_target_pairs={{1,0},{2,1},{3,2},{4,3},{5,4},{6,5},{7,6},{8,7},{9,8},{10,9},{11,1... | collective-permute-start | bytes 1474568 | tf_op jit(solution)/shard_map/ppermute | solution.py:413
  15.1 0.0 copy-start.6
  15.1 0.0 copy-start.7
  15.2 1.9 %collective-permute-start = (f32[1,10,32,128]{3,2,1,0:T(8,128)S(1)}, f32[1,10,32,128]{3,2,1,0:T(8,128)S(1)}, u32[]{:S(2)}, u32[]{:S(2)}) collective-permute-start(f32[1,10,32,128]{3,2,1,0:T(8,128)S(1)} %get-tuple-element.9.up_ref), channel_id=1, source_target_pairs={{0,1},{1,2},{2,3},{3,4},{4,5},{5,6},{6,7},{7,8},{8,9},{9,10},{10,1... | collective-permute-start | bytes 491528 | tf_op jit(solution)/shard_map/ppermute | solution.py:412
  17.1 6.0 %collective-permute-start.1 = (f32[1,10,32,128]{3,2,1,0:T(8,128)S(1)}, f32[1,10,32,128]{3,2,1,0:T(8,128)S(1)}, u32[]{:S(2)}, u32[]{:S(2)}) collective-permute-start(f32[1,10,32,128]{3,2,1,0:T(8,128)S(1)} %get-tuple-element.10.down_ref), channel_id=1, source_target_pairs={{1,0},{2,1},{3,2},{4,3},{5,4},{6,5},{7,6},{8,7},{9,8},{10,9},{11,1... | collective-permute-start | bytes 491528 | tf_op jit(solution)/shard_map/ppermute | solution.py:413
  23.1 4.8 %collective-permute-done.left_ref = f32[1,10,32,128]{3,2,1,0:T(8,128)S(1)} collective-permute-done((f32[1,10,32,128]{3,2,1,0:T(8,128)S(1)}, f32[1,10,32,128]{3,2,1,0:T(8,128)S(1)}, u32[]{:S(2)}, u32[]{:S(2)}) %collective-permute-start) | collective-permute-done | bytes 163872 | tf_op jit(solution)/shard_map/ppermute | solution.py:412
  27.9 1.2 %collective-permute-done.1.right_ref = f32[1,10,32,128]{3,2,1,0:T(8,128)S(1)} collective-permute-done((f32[1,10,32,128]{3,2,1,0:T(8,128)S(1)}, f32[1,10,32,128]{3,2,1,0:T(8,128)S(1)}, u32[]{:S(2)}, u32[]{:S(2)}) %collective-permute-start.1) | collective-permute-done | bytes 163872 | tf_op jit(solution)/shard_map/ppermute | solution.py:413
  29.1 0.0 copy-done.5
  29.1 1.8 %clean.2 = f32[8,1,2,32,128]{4,3,2,1,0:T(8,128)} custom-call(s32[4,16]{1,0:T(4,128)S(1)} %copy-done.5, s32[16]{0:T(128)S(1)} %copy-done.6, s32[16]{0:T(128)S(1)} %copy-done.7, f32[1,10,32,128]{3,2,1,0:T(8,128)S(1)} %collective-permute-done.left_ref, f32[1,10,32,128]{3,2,1,0:T(8,128)S(1)} %get-tuple-element.10.down_ref, ...), custom_call_target="tpu_custom_call" | custom-call | tf_op jit(solution)/shard_map/clean/pallas_call | solution.py:182
  30.9 4.3 %all-to-all-start = ((f32[8,1,2,32,128]{4,3,2,1,0:T(8,128)}), f32[8,1,2,32,128]{4,3,2,1,0:T(8,128)S(1)}, u32[]{:S(2)}, u32[]{:S(2)}) async-start(f32[8,1,2,32,128]{4,3,2,1,0:T(8,128)} %clean.2), calls=%async_computation | async-start | bytes 524288 | tf_op jit(solution)/shard_map/all_to_all | solution.py:418
  35.2 0.0 collective-permute-done.2.left_ref
  35.2 0.0 collective-permute-done.3.right_ref
  35.2 1.8 %clean.3 = f32[8,3,2,32,128]{4,3,2,1,0:T(8,128)S(1)} custom-call(s32[4,16]{1,0:T(4,128)S(1)} %copy-done.5, s32[16]{0:T(128)S(1)} %copy-done.6, s32[16]{0:T(128)S(1)} %copy-done.7, f32[3,10,32,128]{3,2,1,0:T(8,128)S(1)} %collective-permute-done.2.left_ref, f32[3,10,32,128]{3,2,1,0:T(8,128)S(1)} %get-tuple-element.12.down_ref, ...), custom_call_target="tpu_custom_call" | custom-call | tf_op jit(solution)/shard_map/clean/pallas_call | solution.py:182
  37.0 0.0 copy-start
  37.0 0.0 copy-start.1
  37.1 0.0 copy-start.2
  37.1 0.0 copy-start.3
  37.1 0.0 copy-start.4
  37.1 5.6 %all-to-all-done.refs_0_ = f32[8,1,2,32,128]{4,3,2,1,0:T(8,128)S(1)} async-done(((f32[8,1,2,32,128]{4,3,2,1,0:T(8,128)}), f32[8,1,2,32,128]{4,3,2,1,0:T(8,128)S(1)}, u32[]{:S(2)}, u32[]{:S(2)}) %all-to-all-start) | async-done | bytes 262176 | tf_op jit(solution)/shard_map/all_to_all | solution.py:418
  42.7 15.6 %all_to_all.10.refs_1_ = f32[8,3,2,32,128]{4,3,2,1,0:T(8,128)S(1)} all-to-all(f32[8,3,2,32,128]{4,3,2,1,0:T(8,128)S(1)} %clean.3), channel_id=1, replica_groups=mesh['shot'=8,'chan'=64] {'shot'}, dimensions={0} | all-to-all | bytes 1572864 | tf_op jit(solution)/shard_map/all_to_all | solution.py:418
  58.3 3.4 %dip.1 = f32[32,64,128]{2,1,0:T(8,128)} custom-call(s32[16]{0:T(128)} %bands_ref.1, f32[8,1,2,32,128]{4,3,2,1,0:T(8,128)S(1)} %all-to-all-done.refs_0_, f32[8,3,2,32,128]{4,3,2,1,0:T(8,128)S(1)} %all_to_all.10.refs_1_, bf16[64,192]{1,0:T(8,128)(2,1)S(1)} %copy-done.4, bf16[64,192]{1,0:T(8,128)(2,1)S(1)} %copy-done.3, bf16[768,256]{1,0:T(8,128)(2,1)S(1)} %copy-done.1, ...), custom_call_target="tpu_custom_call" | custom-call | tf_op jit(solution)/shard_map/dip/pallas_call | solution.py:387
  (7 shorter events, 0.0 us)
Async XLA Ops:
  1.6 33.6 %collective-permute-start.2 = (f32[3,10,32,128]{3,2,1,0:T(8,128)S(1)}, f32[3,10,32,128]{3,2,1,0:T(8,128)S(1)}, u32[]{:S(2)}, u32[]{:S(2)}) collective-permute-start(f32[3,10,32,128]{3,2,1,0:T(8,128)S(1)} %get-tuple-element.11.up_ref), channel_id=1, source_target_pairs={{0,1},{1,2},{2,3},{3,4},{4,5},{5,6},{6,7},{7,8},{8,9},{9,10},{10,1... | collective-permute-start | bytes 1474568 | tf_op jit(solution)/shard_map/ppermute | solution.py:412
  5.4 23.7 %copy-start.5 = (s32[4,16]{1,0:T(4,128)S(1)}, s32[4,16]{1,0:T(4,128)}, u32[]{:S(2)}) copy-start(s32[4,16]{1,0:T(4,128)} %shifts_ref.5) | copy-start | bytes 772
  5.4 29.7 %collective-permute-start.3 = (f32[3,10,32,128]{3,2,1,0:T(8,128)S(1)}, f32[3,10,32,128]{3,2,1,0:T(8,128)S(1)}, u32[]{:S(2)}, u32[]{:S(2)}) collective-permute-start(f32[3,10,32,128]{3,2,1,0:T(8,128)S(1)} %get-tuple-element.12.down_ref), channel_id=1, source_target_pairs={{1,0},{2,1},{3,2},{4,3},{5,4},{6,5},{7,6},{8,7},{9,8},{10,9},{11,1... | collective-permute-start | bytes 1474568 | tf_op jit(solution)/shard_map/ppermute | solution.py:413
  15.1 14.0 %copy-start.6 = (s32[16]{0:T(128)S(1)}, s32[16]{0:T(128)}, u32[]{:S(2)}) copy-start(s32[16]{0:T(128)} %low_ref.3) | copy-start | bytes 196
  15.1 14.0 %copy-start.7 = (s32[16]{0:T(128)S(1)}, s32[16]{0:T(128)}, u32[]{:S(2)}) copy-start(s32[16]{0:T(128)} %high_ref.3) | copy-start | bytes 196
  15.2 12.8 %collective-permute-start = (f32[1,10,32,128]{3,2,1,0:T(8,128)S(1)}, f32[1,10,32,128]{3,2,1,0:T(8,128)S(1)}, u32[]{:S(2)}, u32[]{:S(2)}) collective-permute-start(f32[1,10,32,128]{3,2,1,0:T(8,128)S(1)} %get-tuple-element.9.up_ref), channel_id=1, source_target_pairs={{0,1},{1,2},{2,3},{3,4},{4,5},{5,6},{6,7},{7,8},{8,9},{9,10},{10,1... | collective-permute-start | bytes 491528 | tf_op jit(solution)/shard_map/ppermute | solution.py:412
  17.1 12.0 %collective-permute-start.1 = (f32[1,10,32,128]{3,2,1,0:T(8,128)S(1)}, f32[1,10,32,128]{3,2,1,0:T(8,128)S(1)}, u32[]{:S(2)}, u32[]{:S(2)}) collective-permute-start(f32[1,10,32,128]{3,2,1,0:T(8,128)S(1)} %get-tuple-element.10.down_ref), channel_id=1, source_target_pairs={{1,0},{2,1},{3,2},{4,3},{5,4},{6,5},{7,6},{8,7},{9,8},{10,9},{11,1... | collective-permute-start | bytes 491528 | tf_op jit(solution)/shard_map/ppermute | solution.py:413
  30.9 11.8 %all-to-all-start = ((f32[8,1,2,32,128]{4,3,2,1,0:T(8,128)}), f32[8,1,2,32,128]{4,3,2,1,0:T(8,128)S(1)}, u32[]{:S(2)}, u32[]{:S(2)}) async-start(f32[8,1,2,32,128]{4,3,2,1,0:T(8,128)} %clean.2), calls=%async_computation | async-start | bytes 524288 | tf_op jit(solution)/shard_map/all_to_all | solution.py:418
  37.0 21.2 %copy-start = (bf16[768,256]{1,0:T(8,128)(2,1)S(1)}, bf16[768,256]{1,0:T(8,128)(2,1)}, u32[]{:S(2)}) copy-start(bf16[768,256]{1,0:T(8,128)(2,1)} %constant.13.clone.refs_5_) | copy-start | bytes 1179652
  37.0 21.2 %copy-start.1 = (bf16[768,256]{1,0:T(8,128)(2,1)S(1)}, bf16[768,256]{1,0:T(8,128)(2,1)}, u32[]{:S(2)}) copy-start(bf16[768,256]{1,0:T(8,128)(2,1)} %constant.12.clone.refs_4_) | copy-start | bytes 1179652
  37.1 21.2 %copy-start.2 = (f32[2,32,128]{2,1,0:T(8,128)S(1)}, f32[2,32,128]{2,1,0:T(8,128)}, u32[]{:S(2)}) copy-start(f32[2,32,128]{2,1,0:T(8,128)} %constant.14.clone.refs_6_) | copy-start | bytes 98308
  37.1 21.2 %copy-start.3 = (bf16[64,192]{1,0:T(8,128)(2,1)S(1)}, bf16[64,192]{1,0:T(8,128)(2,1)}, u32[]{:S(2)}) copy-start(bf16[64,192]{1,0:T(8,128)(2,1)} %constant.11.clone.refs_3_) | copy-start | bytes 73732
  37.1 21.2 %copy-start.4 = (bf16[64,192]{1,0:T(8,128)(2,1)S(1)}, bf16[64,192]{1,0:T(8,128)(2,1)}, u32[]{:S(2)}) copy-start(bf16[64,192]{1,0:T(8,128)(2,1)} %constant.10.clone.refs_2_) | copy-start | bytes 73732

commit v5 on v4

--- a/solution.py
+++ b/solution.py
@@ -135,7 +135,12 @@
     return result
 
 
-def clean_kernel(dims, start, shots_here, shifts_ref, low_ref, high_ref, left_ref, down_ref, up_ref, right_ref, out_ref, held):
+def clean_kernel(dims, start, shots_here, *refs):
+    scalars, (left_ref, down_ref, up_ref, right_ref, out_ref, held), own, sems = refs[:3], refs[3:9], refs[9:12], refs[12]
+    staged = [pltpu.make_async_copy(source, target, sems.at[i]) for i, (source, target) in enumerate(zip(scalars, own))]
+    for copy in staged:
+        copy.start()
+    shifts_ref, low_ref, high_ref = own
     shots, chans, rows = dims
     first_shot = lax.axis_index("shot") * shots_here + start
     lead = 8
@@ -172,6 +177,9 @@
             if shot < shots:
                 passes(shot, part)
             if shot > 0:
+                if shot == 1 and part == 0:
+                    for copy in staged:
+                        copy.wait()
                 for chan in range(part * chans // parts, (part + 1) * chans // parts):
                     restore(shot - 1, chan)
 
@@ -182,9 +190,13 @@
     return pl.pallas_call(
         functools.partial(clean_kernel, (shots, chans, rows), start, shots_here),
         out_shape=jax.ShapeDtypeStruct((groups, shots, chans // groups, rows, LANES), jnp.float32),
-        in_specs=[whole(pltpu.SMEM)] * 3 + [whole()] * 4,
+        in_specs=[whole()] * 7,
         out_specs=whole(),
-        scratch_shapes=[pltpu.VMEM((2, chans, 8 + rows, LANES), jnp.float32)],
+        scratch_shapes=[
+            pltpu.VMEM((2, chans, 8 + rows, LANES), jnp.float32),
+            *(pltpu.SMEM(one.shape, jnp.int32) for one in (shifts, low, high)),
+            pltpu.SemaphoreType.DMA((3,)),
+        ],
         compiler_params=pltpu.CompilerParams(vmem_limit_bytes=GRANT),
         name="clean",
     )(shifts, low, high, left, down, up, right)

time: 62.1 us -> 61.8 us (level)
  Pallas kernels: 8.61 us -> 7.9 us
    pallas_call x2, Pallas kernels: 3.61 us -> 2.9 us  [clean(): pl.pallas_call(functools.partial(clean_kernel, (shots, chans, rows), star...]
  transfers between devices with their start and end apart: 5 -> 5, of which waited for: 3 -> 3; matrix products, arithmetic and copies ran while one was open for 0% -> 0% of each run, Pallas kernels for 6% -> 5%
where the time goes in v5:
time: 61.8 us; the launch traced here: 61.4 us
  starting transfers between devices  25.8 us (42%)
  blocking collectives  15.6 us (25%)
  waiting for transfers between devices  12 us (19%)
  Pallas kernels  7.9 us (13%)
    ppermute x2, starting transfers between devices, local(): right = lax.ppermute(down, 'chan', downward)  15.7 us
    all_to_all x1, blocking collectives, local(): lax.all_to_all(parted, 'shot', split_axis=0, concat_axis=0, tiled=True)  15.6 us
    all_to_all x1, waiting for transfers between devices, local(): lax.all_to_all(parted, 'shot', split_axis=0, concat_axis=0, tiled=True)  5.98 us
    ppermute x2, starting transfers between devices, local(): left = lax.ppermute(up, 'chan', upward)  5.75 us
    ppermute x2, waiting for transfers between devices, local(): left = lax.ppermute(up, 'chan', upward)  4.79 us
    all_to_all x1, starting transfers between devices, local(): lax.all_to_all(parted, 'shot', split_axis=0, concat_axis=0, tiled=True)  4.31 us
    pallas_call x1, Pallas kernels, dip_filter(): pl.pallas_call(functools.partial(dip_kernel, (shots, recs, rows), pieces)...  3.41 us
    pallas_call x2, Pallas kernels, clean(): pl.pallas_call(functools.partial(clean_kernel, (shots, chans, rows), star...  2.9 us
  transfers between devices with their start and end apart: 5, of which 3 were waited for; matrix products, arithmetic and copies ran while one was open for 0% of the time, Pallas kernels for 5%

profile of v5, /device:TPU:24, one launch (start us, length us, event | category | flops | bytes accessed | tf_op | source)
XLA Modules:
  0.0 61.4 jit_solution(5711754193050216485)
XLA Ops:
  0.0 1.6 %align.1 = (f32[1,10,32,128]{3,2,1,0:T(8,128)S(1)}, f32[1,10,32,128]{3,2,1,0:T(8,128)S(1)}, f32[3,10,32,128]{3,2,1,0:T(8,128)S(1)}, f32[3,10,32,128]{3,2,1,0:T(8,128)S(1)}) custom-call(s32[4,16]{1,0:T(4,128)} %refs_0_.3, f32[2048,128]{1,0:T(8,128)} %bitcast.10), custom_call_target="tpu_custom_call" | custom-call | tf_op jit(solution)/shard_map/align/pallas_call | solution.py:68
  1.6 3.8 %collective-permute-start.2 = (f32[3,10,32,128]{3,2,1,0:T(8,128)S(1)}, f32[3,10,32,128]{3,2,1,0:T(8,128)S(1)}, u32[]{:S(2)}, u32[]{:S(2)}) collective-permute-start(f32[3,10,32,128]{3,2,1,0:T(8,128)S(1)} %get-tuple-element.11.refs_5_), channel_id=1, source_target_pairs={{0,1},{1,2},{2,3},{3,4},{4,5},{5,6},{6,7},{7,8},{8,9},{9,10},{10,1... | collective-permute-start | bytes 1474568 | tf_op jit(solution)/shard_map/ppermute | solution.py:424
  5.4 0.0 copy-start.5
  5.4 9.7 %collective-permute-start.3 = (f32[3,10,32,128]{3,2,1,0:T(8,128)S(1)}, f32[3,10,32,128]{3,2,1,0:T(8,128)S(1)}, u32[]{:S(2)}, u32[]{:S(2)}) collective-permute-start(f32[3,10,32,128]{3,2,1,0:T(8,128)S(1)} %get-tuple-element.12.refs_4_), channel_id=1, source_target_pairs={{1,0},{2,1},{3,2},{4,3},{5,4},{6,5},{7,6},{8,7},{9,8},{10,9},{11,1... | collective-permute-start | bytes 1474568 | tf_op jit(solution)/shard_map/ppermute | solution.py:425
  15.1 0.0 copy-start.6
  15.1 0.0 copy-start.7
  15.2 1.9 %collective-permute-start = (f32[1,10,32,128]{3,2,1,0:T(8,128)S(1)}, f32[1,10,32,128]{3,2,1,0:T(8,128)S(1)}, u32[]{:S(2)}, u32[]{:S(2)}) collective-permute-start(f32[1,10,32,128]{3,2,1,0:T(8,128)S(1)} %get-tuple-element.9.refs_5_), channel_id=1, source_target_pairs={{0,1},{1,2},{2,3},{3,4},{4,5},{5,6},{6,7},{7,8},{8,9},{9,10},{10,1... | collective-permute-start | bytes 491528 | tf_op jit(solution)/shard_map/ppermute | solution.py:424
  17.1 6.0 %collective-permute-start.1 = (f32[1,10,32,128]{3,2,1,0:T(8,128)S(1)}, f32[1,10,32,128]{3,2,1,0:T(8,128)S(1)}, u32[]{:S(2)}, u32[]{:S(2)}) collective-permute-start(f32[1,10,32,128]{3,2,1,0:T(8,128)S(1)} %get-tuple-element.10.refs_4_), channel_id=1, source_target_pairs={{1,0},{2,1},{3,2},{4,3},{5,4},{6,5},{7,6},{8,7},{9,8},{10,9},{11,1... | collective-permute-start | bytes 491528 | tf_op jit(solution)/shard_map/ppermute | solution.py:425
  23.1 4.8 %collective-permute-done.refs_3_ = f32[1,10,32,128]{3,2,1,0:T(8,128)S(1)} collective-permute-done((f32[1,10,32,128]{3,2,1,0:T(8,128)S(1)}, f32[1,10,32,128]{3,2,1,0:T(8,128)S(1)}, u32[]{:S(2)}, u32[]{:S(2)}) %collective-permute-start) | collective-permute-done | bytes 163872 | tf_op jit(solution)/shard_map/ppermute | solution.py:424
  27.9 1.2 %collective-permute-done.1.refs_6_ = f32[1,10,32,128]{3,2,1,0:T(8,128)S(1)} collective-permute-done((f32[1,10,32,128]{3,2,1,0:T(8,128)S(1)}, f32[1,10,32,128]{3,2,1,0:T(8,128)S(1)}, u32[]{:S(2)}, u32[]{:S(2)}) %collective-permute-start.1) | collective-permute-done | bytes 163872 | tf_op jit(solution)/shard_map/ppermute | solution.py:425
  29.1 1.5 %clean.2 = f32[8,1,2,32,128]{4,3,2,1,0:T(8,128)} custom-call(s32[4,16]{1,0:T(4,128)S(1)} %copy-done.5, s32[16]{0:T(128)S(1)} %copy-done.6, s32[16]{0:T(128)S(1)} %copy-done.7, f32[1,10,32,128]{3,2,1,0:T(8,128)S(1)} %collective-permute-done.refs_3_, f32[1,10,32,128]{3,2,1,0:T(8,128)S(1)} %get-tuple-element.10.refs_4_, ...), custom_call_target="tpu_custom_call" | custom-call | tf_op jit(solution)/shard_map/clean/pallas_call | solution.py:190
  30.6 4.3 %all-to-all-start = ((f32[8,1,2,32,128]{4,3,2,1,0:T(8,128)}), f32[8,1,2,32,128]{4,3,2,1,0:T(8,128)S(1)}, u32[]{:S(2)}, u32[]{:S(2)}) async-start(f32[8,1,2,32,128]{4,3,2,1,0:T(8,128)} %clean.2), calls=%async_computation | async-start | bytes 524288 | tf_op jit(solution)/shard_map/all_to_all | solution.py:430
  34.9 0.0 collective-permute-done.2.refs_3_
  34.9 0.0 collective-permute-done.3.refs_6_
  34.9 1.4 %clean.3 = f32[8,3,2,32,128]{4,3,2,1,0:T(8,128)S(1)} custom-call(s32[4,16]{1,0:T(4,128)S(1)} %copy-done.5, s32[16]{0:T(128)S(1)} %copy-done.6, s32[16]{0:T(128)S(1)} %copy-done.7, f32[3,10,32,128]{3,2,1,0:T(8,128)S(1)} %collective-permute-done.2.refs_3_, f32[3,10,32,128]{3,2,1,0:T(8,128)S(1)} %get-tuple-element.12.refs_4_, ...), custom_call_target="tpu_custom_call" | custom-call | tf_op jit(solution)/shard_map/clean/pallas_call | solution.py:190
  36.3 0.0 copy-start
  36.4 0.0 copy-start.1
  36.4 0.0 copy-start.2
  36.4 0.0 copy-start.3
  36.4 0.0 copy-start.4
  36.4 6.0 %all-to-all-done.refs_0_ = f32[8,1,2,32,128]{4,3,2,1,0:T(8,128)S(1)} async-done(((f32[8,1,2,32,128]{4,3,2,1,0:T(8,128)}), f32[8,1,2,32,128]{4,3,2,1,0:T(8,128)S(1)}, u32[]{:S(2)}, u32[]{:S(2)}) %all-to-all-start) | async-done | bytes 262176 | tf_op jit(solution)/shard_map/all_to_all | solution.py:430
  42.4 15.6 %all_to_all.10.refs_1_ = f32[8,3,2,32,128]{4,3,2,1,0:T(8,128)S(1)} all-to-all(f32[8,3,2,32,128]{4,3,2,1,0:T(8,128)S(1)} %clean.3), channel_id=1, replica_groups=mesh['shot'=8,'chan'=64] {'shot'}, dimensions={0} | all-to-all | bytes 1572864 | tf_op jit(solution)/shard_map/all_to_all | solution.py:430
  58.0 0.0 copy-done.1
  58.0 3.4 %dip.1 = f32[32,64,128]{2,1,0:T(8,128)} custom-call(s32[16]{0:T(128)} %bands_ref.1, f32[8,1,2,32,128]{4,3,2,1,0:T(8,128)S(1)} %all-to-all-done.refs_0_, f32[8,3,2,32,128]{4,3,2,1,0:T(8,128)S(1)} %all_to_all.10.refs_1_, bf16[64,192]{1,0:T(8,128)(2,1)S(1)} %copy-done.4, bf16[64,192]{1,0:T(8,128)(2,1)S(1)} %copy-done.3, bf16[768,256]{1,0:T(8,128)(2,1)S(1)} %copy-done.1, ...), custom_call_target="tpu_custom_call" | custom-call | tf_op jit(solution)/shard_map/dip/pallas_call | solution.py:399
  (7 shorter events, 0.0 us)
Async XLA Ops:
  1.6 33.3 %collective-permute-start.2 = (f32[3,10,32,128]{3,2,1,0:T(8,128)S(1)}, f32[3,10,32,128]{3,2,1,0:T(8,128)S(1)}, u32[]{:S(2)}, u32[]{:S(2)}) collective-permute-start(f32[3,10,32,128]{3,2,1,0:T(8,128)S(1)} %get-tuple-element.11.refs_5_), channel_id=1, source_target_pairs={{0,1},{1,2},{2,3},{3,4},{4,5},{5,6},{6,7},{7,8},{8,9},{9,10},{10,1... | collective-permute-start | bytes 1474568 | tf_op jit(solution)/shard_map/ppermute | solution.py:424
  5.4 23.7 %copy-start.5 = (s32[4,16]{1,0:T(4,128)S(1)}, s32[4,16]{1,0:T(4,128)}, u32[]{:S(2)}) copy-start(s32[4,16]{1,0:T(4,128)} %refs_0_.3) | copy-start | bytes 772
  5.4 29.5 %collective-permute-start.3 = (f32[3,10,32,128]{3,2,1,0:T(8,128)S(1)}, f32[3,10,32,128]{3,2,1,0:T(8,128)S(1)}, u32[]{:S(2)}, u32[]{:S(2)}) collective-permute-start(f32[3,10,32,128]{3,2,1,0:T(8,128)S(1)} %get-tuple-element.12.refs_4_), channel_id=1, source_target_pairs={{1,0},{2,1},{3,2},{4,3},{5,4},{6,5},{7,6},{8,7},{9,8},{10,9},{11,1... | collective-permute-start | bytes 1474568 | tf_op jit(solution)/shard_map/ppermute | solution.py:425
  15.1 14.0 %copy-start.6 = (s32[16]{0:T(128)S(1)}, s32[16]{0:T(128)}, u32[]{:S(2)}) copy-start(s32[16]{0:T(128)} %refs_1_.3) | copy-start | bytes 196
  15.1 14.0 %copy-start.7 = (s32[16]{0:T(128)S(1)}, s32[16]{0:T(128)}, u32[]{:S(2)}) copy-start(s32[16]{0:T(128)} %refs_2_.4) | copy-start | bytes 196
  15.2 12.8 %collective-permute-start = (f32[1,10,32,128]{3,2,1,0:T(8,128)S(1)}, f32[1,10,32,128]{3,2,1,0:T(8,128)S(1)}, u32[]{:S(2)}, u32[]{:S(2)}) collective-permute-start(f32[1,10,32,128]{3,2,1,0:T(8,128)S(1)} %get-tuple-element.9.refs_5_), channel_id=1, source_target_pairs={{0,1},{1,2},{2,3},{3,4},{4,5},{5,6},{6,7},{7,8},{8,9},{9,10},{10,1... | collective-permute-start | bytes 491528 | tf_op jit(solution)/shard_map/ppermute | solution.py:424
  17.1 12.0 %collective-permute-start.1 = (f32[1,10,32,128]{3,2,1,0:T(8,128)S(1)}, f32[1,10,32,128]{3,2,1,0:T(8,128)S(1)}, u32[]{:S(2)}, u32[]{:S(2)}) collective-permute-start(f32[1,10,32,128]{3,2,1,0:T(8,128)S(1)} %get-tuple-element.10.refs_4_), channel_id=1, source_target_pairs={{1,0},{2,1},{3,2},{4,3},{5,4},{6,5},{7,6},{8,7},{9,8},{10,9},{11,1... | collective-permute-start | bytes 491528 | tf_op jit(solution)/shard_map/ppermute | solution.py:425
  30.6 11.8 %all-to-all-start = ((f32[8,1,2,32,128]{4,3,2,1,0:T(8,128)}), f32[8,1,2,32,128]{4,3,2,1,0:T(8,128)S(1)}, u32[]{:S(2)}, u32[]{:S(2)}) async-start(f32[8,1,2,32,128]{4,3,2,1,0:T(8,128)} %clean.2), calls=%async_computation | async-start | bytes 524288 | tf_op jit(solution)/shard_map/all_to_all | solution.py:430
  36.3 21.6 %copy-start = (bf16[768,256]{1,0:T(8,128)(2,1)S(1)}, bf16[768,256]{1,0:T(8,128)(2,1)}, u32[]{:S(2)}) copy-start(bf16[768,256]{1,0:T(8,128)(2,1)} %constant.13.clone.refs_5_) | copy-start | bytes 1179652
  36.4 21.6 %copy-start.1 = (bf16[768,256]{1,0:T(8,128)(2,1)S(1)}, bf16[768,256]{1,0:T(8,128)(2,1)}, u32[]{:S(2)}) copy-start(bf16[768,256]{1,0:T(8,128)(2,1)} %constant.12.clone.refs_4_) | copy-start | bytes 1179652
  36.4 21.6 %copy-start.2 = (f32[2,32,128]{2,1,0:T(8,128)S(1)}, f32[2,32,128]{2,1,0:T(8,128)}, u32[]{:S(2)}) copy-start(f32[2,32,128]{2,1,0:T(8,128)} %constant.14.clone.refs_6_) | copy-start | bytes 98308
  36.4 21.6 %copy-start.3 = (bf16[64,192]{1,0:T(8,128)(2,1)S(1)}, bf16[64,192]{1,0:T(8,128)(2,1)}, u32[]{:S(2)}) copy-start(bf16[64,192]{1,0:T(8,128)(2,1)} %constant.11.clone.refs_3_) | copy-start | bytes 73732
  36.4 21.6 %copy-start.4 = (bf16[64,192]{1,0:T(8,128)(2,1)S(1)}, bf16[64,192]{1,0:T(8,128)(2,1)}, u32[]{:S(2)}) copy-start(bf16[64,192]{1,0:T(8,128)(2,1)} %constant.10.clone.refs_2_) | copy-start | bytes 73732
